TPU v7x, 512 devices: a whole 4x8x8 slice. The times are simulated.
512 devices in a mesh: slab: 8 (over y), orb: 64 (over x, z, core).
Axes of the slice: x: 4, y: 8, z: 8, core: 2. Of those that a mesh axis runs over, the one named last changes fastest.
Arguments:
- orbitals_t: bfloat16 [2048, 65536], P('orb', 'slab'), may hold values from -6 to 6
- tiles: bfloat16 [896, 128, 128], P('slab'), may hold values from -0.375 to 0.375
- tile_rows: int32 [896], P('slab'), may hold values from 0 to 63
- tile_cols: int32 [896], P('slab'), may hold values from -2 to 65, as said below
- row_counts: int32 [512], P('slab'), may hold values from 1 to 128, 49152 in all
- bounds: float32 [3], replicated, may hold values from 0 to 1
- rotation: bfloat16 [2048, 2048], P('orb'), may hold values from -0.125 to 0.125
Outputs:
- rotated_t: bfloat16 [2048, 65536], P('orb', 'slab')
Inputs may be any that keep to these rules, and one draw needn't show every extreme that they name: `tile_cols`: within every slab, the first 64 tiles are the diagonal tiles of row blocks 0 to 63 in order; a tile's column block lies within 2 blocks of its row block; in every slab some tile of row block 0 has column block -2 and some tile of row block 63 has column block 65.
All inputs are finite; a program needn't handle non-finite values. No bound on the sum of `row_counts` on one device may be relied on, other than what follows from the above.
Results may differ from a plain program's by a relative error of at most 0.006.
Values may be sent and summed in bfloat16 or wider, within the bound.
A program may use at most 64 MiB of HBM per device.

v0:
```python
import jax
import jax.numpy as jnp
from jax import lax
from jax.sharding import PartitionSpec as P

HB = 2


def with_halo(block, sides, width):
    for axis, dim in sides:
        count = lax.axis_size(axis)
        forward = [(i, i + 1) for i in range(count - 1)]
        backward = [(target, source) for source, target in forward]
        low = lax.ppermute(
            lax.slice_in_dim(block, block.shape[dim] - width, None, axis=dim), axis, forward
        )
        high = lax.ppermute(lax.slice_in_dim(block, 0, width, axis=dim), axis, backward)
        block = jnp.concatenate([low, block, high], axis=dim)
    return block


def local(orbitals_t, tiles, tile_rows, tile_cols, row_counts, bounds, rotation):
    norb_dev, rows_dev = orbitals_t.shape
    tile_size = tiles.shape[1]
    blocks = rows_dev // tile_size
    lower_bound = -3.0 + bounds[0]
    cutoff = bounds[1] - 0.5
    upper_bound = 3.0 + bounds[2]
    half_width = (upper_bound - cutoff) / 2.0
    center = (upper_bound + cutoff) / 2.0
    sigma_one = half_width / (lower_bound - center)
    sigma_two = 1.0 / (2.0 / sigma_one - sigma_one)
    live = (
        (lax.broadcasted_iota(jnp.int32, (blocks, tile_size), 1) < row_counts[:, None])
        .astype(jnp.float32)
        .reshape(rows_dev)
    )
    extra_rows = tile_rows[blocks:]
    onehot = (extra_rows[:, None] == lax.broadcasted_iota(jnp.int32, (1, blocks), 1)).astype(
        jnp.float32
    )
    col_index = tile_cols + HB

    def apply_tiles(source):
        extended = with_halo(source, (("slab", 1),), HB * tile_size)
        col_blocks = extended.reshape(norb_dev, blocks + 2 * HB, tile_size)
        picked = jnp.take(col_blocks, col_index, axis=1)
        products = jnp.einsum("otc,trc->otr", picked, tiles, preferred_element_type=jnp.float32)
        diagonal_part = products[:, :blocks]
        extra_part = jnp.einsum(
            "otr,tb->obr", products[:, blocks:], onehot, precision=lax.Precision.HIGH
        )
        summed = diagonal_part + extra_part
        return summed.reshape(norb_dev, rows_dev)

    source = orbitals_t.astype(jnp.float32)
    applied = apply_tiles(orbitals_t)
    filtered_one = (live * (applied - center * source) * (sigma_one / half_width)).astype(
        jnp.bfloat16
    )
    applied = apply_tiles(filtered_one)
    first = filtered_one.astype(jnp.float32)
    filtered_two = (
        live
        * (
            (applied - center * first) * (2.0 * sigma_two / half_width)
            - sigma_one * sigma_two * source
        )
    ).astype(jnp.bfloat16)
    row_major = lax.all_to_all(filtered_two, "orb", split_axis=1, concat_axis=0, tiled=True)
    rotated = jnp.einsum(
        "kj,kr->jr",
        lax.all_gather(rotation, "orb", axis=0, tiled=True),
        row_major,
        preferred_element_type=jnp.float32,
    ).astype(jnp.bfloat16)
    return lax.all_to_all(rotated, "orb", split_axis=0, concat_axis=1, tiled=True)


def solution(mesh):
    return jax.shard_map(
        local,
        mesh=mesh,
        in_specs=(
            P("orb", "slab"),
            P("slab", None, None),
            P("slab"),
            P("slab"),
            P("slab"),
            P(),
            P("orb", None),
        ),
        out_specs=P("orb", "slab"),
        check_vma=False,
    )
```

profile of v0, /device:TPU:1, one launch (start us, length us, event | category | flops | bytes accessed | tf_op | source)
XLA Modules:
  0.0 141.2 jit_solution(16614028863514410345)
XLA Ops:
  6.5 0.0 all-gather.2.cloned.1.call-start
  6.5 0.7 all-gather.2.cloned.1.call-update
  7.3 0.7 fusion.32
  8.0 4.0 %collective-permute-start = (bf16[32,256]{1,0:T(8,128)(2,1)S(1)}, bf16[32,256]{1,0:T(8,128)(2,1)S(1)}, u32[]{:S(2)}, u32[]{:S(2)}) collective-permute-start(bf16[32,256]{1,0:T(8,128)(2,1)S(1)} %get-tuple-element.10), channel_id=1, source_target_pairs={{0,64},{64,128},{128,192},{192,256},{256,320},{320,384},{384,448},... | collective-permute-start | bytes 49160 | tf_op jit(solution)/shard_map/ppermute | solution.py:14
  12.0 1.3 collective-permute-start.1
  13.3 1.4 %fusion.33 = (f32[1]{0:T(128)}, f32[1]{0:T(128)}, f32[1]{0:T(128)}) fusion(f32[3]{0:T(128)} %param.14), kind=kLoop, calls=%fused_computation.53 | loop fusion | bytes 24 | tf_op jit(solution)/shard_map/slice | solution.py:26
  14.7 0.7 compare_and_fusion
  15.4 0.7 convert_bitcast_fusion
  18.1 0.7 slice.39
  18.8 0.0 collective-permute-done
  18.8 0.0 collective-permute-done.1
  18.8 1.1 copy_bitcast_fusion.1
  20.0 0.7 gather_fusion
  20.7 4.1 %convolution_bitcast_fusion.1 = f32[32,112,128]{2,0,1:T(8,128)S(1)} fusion(bf16[112,128,128]{2,1,0:T(8,128)(2,1)} %param.10, bf16[112,32,128]{2,1,0:T(8,128)(2,1)S(1)} %gather_fusion, pred[112]{0:T(512)(128)(4,1)S(1)} %get-tuple-element.6), kind=kOutput, calls=%fused_computation.5 | convolution fusion | flops 117899264 | bytes 6422640 | tf_op jit(solution)/shard_map/otc,trc->otr/dot_general | solution.py:48
  24.8 0.0 copy-start
  24.8 0.1 slice.53
  24.9 0.9 fusion.19
  25.8 0.1 copy-done
  25.9 0.7 fusion.4
  26.6 4.0 %collective-permute-start.2 = (bf16[32,256]{1,0:T(8,128)(2,1)S(1)}, bf16[32,256]{1,0:T(8,128)(2,1)S(1)}, u32[]{:S(2)}, u32[]{:S(2)}) collective-permute-start(bf16[32,256]{1,0:T(8,128)(2,1)S(1)} %get-tuple-element.8), channel_id=1, source_target_pairs={{0,64},{64,128},{128,192},{192,256},{256,320},{320,384},{384,448},... | collective-permute-start | bytes 49160 | tf_op jit(solution)/shard_map/ppermute | solution.py:14
  30.6 1.3 collective-permute-start.3
  32.1 0.0 collective-permute-done.2
  32.1 3.4 %collective-permute-done.3 = bf16[32,256]{1,0:T(8,128)(2,1)S(1)} collective-permute-done((bf16[32,256]{1,0:T(8,128)(2,1)S(1)}, bf16[32,256]{1,0:T(8,128)(2,1)S(1)}, u32[]{:S(2)}, u32[]{:S(2)}) %collective-permute-start.3) | collective-permute-done | bytes 16416 | tf_op jit(solution)/shard_map/ppermute | solution.py:17
  35.5 0.1 copy_bitcast_fusion
  35.6 0.7 gather_fusion.1
  36.3 4.1 %convolution_bitcast_fusion = f32[32,112,128]{2,0,1:T(8,128)S(1)} fusion(bf16[112,128,128]{2,1,0:T(8,128)(2,1)} %param.10, bf16[112,32,128]{2,1,0:T(8,128)(2,1)S(1)} %gather_fusion.1, pred[112]{0:T(512)(128)(4,1)S(1)} %get-tuple-element.6), kind=kOutput, calls=%fused_computation.4 | convolution fusion | flops 117899264 | bytes 6422640 | tf_op jit(solution)/shard_map/otc,trc->otr/dot_general | solution.py:48
  40.5 0.1 slice.57
  40.5 0.9 fusion.17
  41.4 0.8 copy_bitcast_fusion.3
  42.2 32.7 %all_to_all.38 = bf16[32,64,128]{2,0,1:T(8,128)(2,1)S(1)} all-to-all(bf16[32,64,128]{2,0,1:T(8,128)(2,1)S(1)} %copy_bitcast_fusion.3), channel_id=1, replica_groups=mesh['slab'=8,'orb'=64] {'orb'}, dimensions={1} | all-to-all | bytes 1048576 | tf_op jit(solution)/shard_map/all_to_all | solution.py:70
  74.9 30.9 %all-gather.2.cloned.1.call-done = bf16[2048,2048]{1,0:T(8,128)(2,1)} async-done(((bf16[32,2048]{1,0:T(8,128)(2,1)}), bf16[2048,2048]{1,0:T(8,128)(2,1)}) %all-gather.2.cloned.1.call-update) | async-done | bytes 8388624 | tf_op jit(solution)/shard_map/all_gather | solution.py:73
  105.9 4.7 %fusion = bf16[2048,128]{0,1:T(8,128)(2,1)S(1)} fusion(bf16[2048,128]{1,0:T(8,128)(2,1)S(1)} %bitcast.75, bf16[2048,2048]{1,0:T(8,128)(2,1)} %all-gather.2.cloned.1.call-done), kind=kOutput, calls=%fused_computation.3 | convolution fusion | flops 1074003968 | bytes 9437184 | tf_op jit(solution)/shard_map/kj,kr->jr/dot_general | solution.py:71
  110.5 0.3 copy.32
  110.8 22.7 %all_to_all.39 = bf16[64,32,128]{2,1,0:T(8,128)(2,1)S(1)} all-to-all(bf16[64,32,128]{2,1,0:T(8,128)(2,1)S(1)} %bitcast.76), channel_id=1, replica_groups=mesh['slab'=8,'orb'=64] {'orb'}, dimensions={0} | all-to-all | bytes 1048576 | tf_op jit(solution)/shard_map/all_to_all | solution.py:77
  133.5 0.8 copy_bitcast_fusion.2
  (2 shorter events, 0.0 us)
Async XLA Ops:
  6.5 99.3 %all-gather.2.cloned.1.call-start = ((), (), s32[]{:S(2)}) async-start(), calls=%async_computation.2 | async-start | bytes 8519680 | tf_op jit(solution)/shard_map/all_gather | solution.py:73
  8.0 10.8 %collective-permute-start = (bf16[32,256]{1,0:T(8,128)(2,1)S(1)}, bf16[32,256]{1,0:T(8,128)(2,1)S(1)}, u32[]{:S(2)}, u32[]{:S(2)}) collective-permute-start(bf16[32,256]{1,0:T(8,128)(2,1)S(1)} %get-tuple-element.10), channel_id=1, source_target_pairs={{0,64},{64,128},{128,192},{192,256},{256,320},{320,384},{384,448},... | collective-permute-start | bytes 49160 | tf_op jit(solution)/shard_map/ppermute | solution.py:14
  12.0 6.8 %collective-permute-start.1 = (bf16[32,256]{1,0:T(8,128)(2,1)S(1)}, bf16[32,256]{1,0:T(8,128)(2,1)S(1)}, u32[]{:S(2)}, u32[]{:S(2)}) collective-permute-start(bf16[32,256]{1,0:T(8,128)(2,1)S(1)} %get-tuple-element.11), channel_id=1, source_target_pairs={{64,0},{128,64},{192,128},{256,192},{320,256},{384,320},{448,384},... | collective-permute-start | bytes 49160 | tf_op jit(solution)/shard_map/ppermute | solution.py:17
  24.8 1.1 copy-start
  26.6 5.5 %collective-permute-start.2 = (bf16[32,256]{1,0:T(8,128)(2,1)S(1)}, bf16[32,256]{1,0:T(8,128)(2,1)S(1)}, u32[]{:S(2)}, u32[]{:S(2)}) collective-permute-start(bf16[32,256]{1,0:T(8,128)(2,1)S(1)} %get-tuple-element.8), channel_id=1, source_target_pairs={{0,64},{64,128},{128,192},{192,256},{256,320},{320,384},{384,448},... | collective-permute-start | bytes 49160 | tf_op jit(solution)/shard_map/ppermute | solution.py:14
  30.6 4.9 %collective-permute-start.3 = (bf16[32,256]{1,0:T(8,128)(2,1)S(1)}, bf16[32,256]{1,0:T(8,128)(2,1)S(1)}, u32[]{:S(2)}, u32[]{:S(2)}) collective-permute-start(bf16[32,256]{1,0:T(8,128)(2,1)S(1)} %get-tuple-element.9), channel_id=1, source_target_pairs={{64,0},{128,64},{192,128},{256,192},{320,256},{384,320},{448,384},... | collective-permute-start | bytes 49160 | tf_op jit(solution)/shard_map/ppermute | solution.py:17
Sparse Core Ops, SparseCore 0:
  10.7 95.1 all-gather.1
where the time goes:
time: 142 us; the launch traced here: 141 us
  blocking collectives  55.4 us (39%)
  waiting for transfers between devices  35.1 us (25%)
  between operations  15.6 us (11%)
  matrix products  14.7 us (10%)
  starting transfers between devices  10.6 us (7%)
  local copies, waits for them, and re-layouts  5.69 us (4%)
  other arithmetic  4.15 us (3%)
    all_to_all x1, blocking collectives, local(): lax.all_to_all(filtered_two, 'orb', split_axis=1, concat_axis=0, tiled=True)  32.7 us
    all_gather x1, waiting for transfers between devices, local(): lax.all_gather(rotation, 'orb', axis=0, tiled=True)  30.9 us
    all_to_all x1, blocking collectives, local(): lax.all_to_all(rotated, 'orb', split_axis=0, concat_axis=1, tiled=True)  22.7 us
    dot_general x2, matrix products, apply_tiles(): jnp.einsum('otc,trc->otr', picked, tiles, preferred_element_type=jnp.floa...  8.23 us
    ppermute x2, starting transfers between devices, with_halo(): lax.ppermute(lax.slice_in_dim(block, block.shape[dim] - width, None, axis...  7.99 us
    dot_general x1, matrix products, local(): jnp.einsum('kj,kr->jr', lax.all_gather(rotation, 'orb', axis=0, tiled=Tru...  4.66 us
    ppermute x2, waiting for transfers between devices, with_halo(): lax.ppermute(lax.slice_in_dim(block, 0, width, axis=dim), axis, backward)  3.41 us
  transfers between devices with their start and end apart: 5, of which 2 were waited for; matrix products, arithmetic and copies ran while one was open for 13% of the time, Pallas kernels for 0%

commit v1 on v0

--- a/solution.py
+++ b/solution.py
@@ -1,9 +1,238 @@
+import functools
+
 import jax
 import jax.numpy as jnp
 from jax import lax
+from jax.experimental import pallas as pl
+from jax.experimental.pallas import tpu as pltpu
 from jax.sharding import PartitionSpec as P
 
 HB = 2
+NX, NZ = 4, 8
+CHIPS = NX * NZ
+NORB_DEV = 32
+TILE = 128
+PAIR = 2 * TILE
+STEPS = 4
+MESH = pl.DeviceIdType.MESH
+BF16 = jnp.bfloat16
+
+
+def column_group(core, half, step, z):
+    owner_x = 2 * core + lax.rem(step + z, 2)
+    z_pair = half + 2 * lax.rem(step // 2 + z // 2, 2)
+    return owner_x * 4 + z_pair
+
+
+def rotate_kernel(
+    f2_hbm, r_hbm, out_hbm,
+    f2, rv, rb, fb, ft, ob, ov,
+    in_sem, z_send, z_recv, x_send, x_recv, y_send, y_recv,
+    f_send, f_recv, g_send, g_recv, o_send, o_recv, out_sem,
+):
+    s, o = lax.axis_index("slab"), lax.axis_index("orb")
+    n_slab, n_orb = 8, 64
+    core, chip = lax.rem(o, 2), o // 2
+    z, x = lax.rem(chip, NZ), chip // NZ
+    half = lax.rem(s, 2)
+    partner = o + 1 - 2 * core
+    x_up, x_down = lax.rem(x + 1, NX), lax.rem(x + NX - 1, NX)
+    x_far = lax.rem(x + 2, NX)
+    s_up, s_down = lax.rem(s + 1, n_slab), lax.rem(s + n_slab - 1, n_slab)
+
+    load_r = pltpu.make_async_copy(r_hbm, rv, in_sem.at[0])
+    load_r.start()
+    load_f = pltpu.make_async_copy(f2_hbm, f2, in_sem.at[1])
+    load_f.start()
+
+    barrier = pltpu.get_barrier_semaphore()
+
+    def greet(i, carry):
+        pl.semaphore_signal(barrier, inc=1, device_id=(s, lax.rem(o + i, n_orb)), device_id_type=MESH)
+        return carry
+
+    lax.fori_loop(1, n_orb, greet, 0)
+    for other in (s_up, s_down):
+        pl.semaphore_signal(barrier, inc=1, device_id=(other, o), device_id_type=MESH)
+    load_r.wait()
+    load_f.wait()
+    pl.semaphore_wait(barrier, n_orb - 1 + 2)
+
+    def send(src, dst, send_sem, recv_sem, to):
+        pltpu.make_async_remote_copy(
+            src_ref=src, dst_ref=dst, send_sem=send_sem, recv_sem=recv_sem,
+            device_id=to, device_id_type=MESH,
+        ).start()
+
+    def wait_bytes(ref, sem):
+        pltpu.make_async_copy(ref, ref, sem).wait()
+
+    def rotation_columns(to_core, step, to_z):
+        first = column_group(to_core, half, step, to_z) * TILE
+        return rv.at[:, pl.ds(pl.multiple_of(first, TILE), TILE)]
+
+    def z_step(step, carry):
+        pltpu.make_async_copy(
+            rotation_columns(core, step, z), rb.at[half, step, core, chip], z_recv.at[step]
+        ).start()
+
+        def one(i, inner):
+            there = lax.rem(z * 2 + core + i, 2 * NZ)
+            send(
+                rotation_columns(lax.rem(there, 2), step, there // 2),
+                rb.at[half, step, core, chip], z_send, z_recv.at[step], (s, x * 2 * NZ + there),
+            )
+            return inner
+
+        lax.fori_loop(1, 2 * NZ, one, 0)
+        return carry
+
+    lax.fori_loop(0, STEPS, z_step, 0)
+
+    pltpu.make_async_copy(
+        f2.at[:, pl.ds(pl.multiple_of(chip * PAIR, PAIR), PAIR)], fb.at[core, chip], f_recv.at[x]
+    ).start()
+
+    def f_one(i, carry):
+        there = lax.rem(chip + i, CHIPS)
+        send(
+            f2.at[:, pl.ds(pl.multiple_of(there * PAIR, PAIR), PAIR)],
+            fb.at[core, chip], f_send, f_recv.at[x], (s, there * 2 + core),
+        )
+        return carry
+
+    lax.fori_loop(1, CHIPS, f_one, 0)
+
+    def of_x(step, which, at_x):
+        return rb.at[which, step, :, pl.ds(at_x * NZ, NZ)]
+
+    def of_x_core(step, which, at_core, at_x):
+        return rb.at[which, step, at_core, pl.ds(at_x * NZ, NZ)]
+
+    def to_slabs(step, at_x):
+        send(of_x_core(step, half, 0, at_x), of_x_core(step, half, 0, at_x), y_send, y_recv.at[step], (s_up, o))
+        send(of_x_core(step, half, 1, at_x), of_x_core(step, half, 1, at_x), y_send, y_recv.at[step], (s_down, o))
+
+    def orb_at(at_x):
+        return (at_x * NZ + z) * 2 + core
+
+    def stage_one(step, carry):
+        mine = of_x(step, half, x)
+        wait_bytes(mine, z_recv.at[step])
+        send(mine, mine, x_send, x_recv.at[step, 0], (s, orb_at(x_up)))
+        send(mine, mine, x_send, x_recv.at[step, 1], (s, orb_at(x_down)))
+        to_slabs(step, x)
+        return carry
+
+    def stage_two(step, carry):
+        wait_bytes(of_x(step, half, x_down), x_recv.at[step, 0])
+        relayed = of_x_core(step, half, 0, x_down)
+        send(relayed, relayed, x_send, x_recv.at[step, 2], (s, orb_at(x_up)))
+        wait_bytes(of_x(step, half, x_up), x_recv.at[step, 1])
+        relayed = of_x_core(step, half, 1, x_up)
+        send(relayed, relayed, x_send, x_recv.at[step, 3], (s, orb_at(x_down)))
+        to_slabs(step, x_down)
+        to_slabs(step, x_up)
+        return carry
+
+    def stage_three(step, carry):
+        wait_bytes(of_x_core(step, half, 0, x_far), x_recv.at[step, 2])
+        wait_bytes(of_x_core(step, half, 1, x_far), x_recv.at[step, 3])
+        to_slabs(step, x_far)
+        return carry
+
+    lax.fori_loop(0, STEPS, stage_one, 0)
+    lax.fori_loop(0, STEPS, stage_two, 0)
+
+    def pass_on(at_x, carry):
+        got = fb.at[core, pl.ds(at_x * NZ, NZ)]
+        wait_bytes(got, f_recv.at[at_x])
+        send(got, got, g_send, g_recv.at[at_x], (s, partner))
+        return carry
+
+    lax.fori_loop(0, NX, pass_on, 0)
+    lax.fori_loop(0, STEPS, stage_three, 0)
+
+    def wait_partner(at_x, carry):
+        wait_bytes(fb.at[1 - core, pl.ds(at_x * NZ, NZ)], g_recv.at[at_x])
+        return carry
+
+    lax.fori_loop(0, NX, wait_partner, 0)
+
+    for at_core in range(2):
+        for group in range(CHIPS // 4):
+            block = fb[at_core, 4 * group:4 * group + 4].reshape(TILE, PAIR)
+            first = at_core * CHIPS * NORB_DEV + group * TILE
+            ft[:, first:first + TILE] = block.T
+
+    def rotate(step, which):
+        slot = rb[which, step].reshape(2 * CHIPS * NORB_DEV, TILE)
+        made = jnp.dot(ft[...], slot, preferred_element_type=jnp.float32)
+        ob[which, step] = made.T.astype(BF16)
+        first = column_group(core, which, step, z) * 4
+        columns = pl.ds(pl.multiple_of(chip * PAIR, PAIR), PAIR)
+        for i in range(4):
+            piece = ob.at[which, step, pl.ds(i * NORB_DEV, NORB_DEV)]
+
+            @pl.when(first + i == o)
+            def _():
+                pltpu.make_async_copy(piece, ov.at[:, columns], o_recv).start()
+
+            @pl.when(first + i != o)
+            def _():
+                send(piece, ov.at[:, columns], o_send, o_recv, (s, first + i))
+
+    def finish(step, carry):
+        rotate(step, half)
+        wait_bytes(rb.at[1 - half, step], y_recv.at[step])
+        rotate(step, 1 - half)
+        return carry
+
+    lax.fori_loop(0, STEPS, finish, 0)
+
+    wait_bytes(ov, o_recv)
+    store = pltpu.make_async_copy(ov, out_hbm, out_sem)
+    store.start()
+    wait_bytes(rb.at[0, 0, :, pl.ds(0, 30)], z_send)
+    wait_bytes(rb.at[0, pl.ds(0, 3)], x_send)
+    wait_bytes(rb.at[0], y_send)
+    wait_bytes(fb.at[0, pl.ds(0, CHIPS - 1)], f_send)
+    wait_bytes(fb.at[0], g_send)
+
+    @pl.when(x // 2 == core)
+    def _():
+        wait_bytes(fb.at[0, pl.ds(0, CHIPS - 1)], o_send)
+
+    @pl.when(x // 2 != core)
+    def _():
+        wait_bytes(fb.at[0], o_send)
+
+    store.wait()
+
+
+def rotate(filtered, rotation):
+    rows = filtered.shape[1]
+    dma = pltpu.SemaphoreType.DMA
+    return pl.pallas_call(
+        rotate_kernel,
+        out_shape=jax.ShapeDtypeStruct(filtered.shape, BF16),
+        in_specs=[pl.BlockSpec(memory_space=pl.ANY)] * 2,
+        out_specs=pl.BlockSpec(memory_space=pl.ANY),
+        scratch_shapes=[
+            pltpu.VMEM((NORB_DEV, rows), BF16),
+            pltpu.VMEM(rotation.shape, BF16),
+            pltpu.VMEM((2, STEPS, 2, CHIPS, NORB_DEV, TILE), BF16),
+            pltpu.VMEM((2, CHIPS, NORB_DEV, PAIR), BF16),
+            pltpu.VMEM((PAIR, 2 * CHIPS * NORB_DEV), BF16),
+            pltpu.VMEM((2, STEPS, TILE, PAIR), BF16),
+            pltpu.VMEM((NORB_DEV, rows), BF16),
+            dma((2,)), dma, dma((STEPS,)), dma, dma((STEPS, 4)), dma, dma((STEPS,)),
+            dma, dma((NX,)), dma, dma((NX,)), dma, dma, dma,
+        ],
+        compiler_params=pltpu.CompilerParams(
+            collective_id=0, has_side_effects=True, vmem_limit_bytes=40 << 20
+        ),
+    )(filtered, rotation)
 
 
 def with_halo(block, sides, width):
@@ -67,14 +296,7 @@
             - sigma_one * sigma_two * source
         )
     ).astype(jnp.bfloat16)
-    row_major = lax.all_to_all(filtered_two, "orb", split_axis=1, concat_axis=0, tiled=True)
-    rotated = jnp.einsum(
-        "kj,kr->jr",
-        lax.all_gather(rotation, "orb", axis=0, tiled=True),
-        row_major,
-        preferred_element_type=jnp.float32,
-    ).astype(jnp.bfloat16)
-    return lax.all_to_all(rotated, "orb", split_axis=0, concat_axis=1, tiled=True)
+    return rotate(filtered_two, rotation)
 
 
 def solution(mesh):

time: 142 us -> 102 us (0.72)
  the two profiles are of different devices: /device:TPU:1 before, /device:TPU:25 now
where the time goes in v1:
time: 102 us
  Pallas kernels  63.2 us (62%)
  starting transfers between devices  12.8 us (13%)
  matrix products  9.95 us (10%)
  local copies, waits for them, and re-layouts  5.48 us (5%)
  other arithmetic  4.15 us (4%)
  waiting for transfers between devices  3.59 us (4%)
  between operations  2.28 us (2%)
    pallas_call x1, Pallas kernels, rotate(): pl.pallas_call(rotate_kernel, out_shape=jax.ShapeDtypeStruct(filtered.sha...  63.2 us
    ppermute x2, starting transfers between devices, with_halo(): lax.ppermute(lax.slice_in_dim(block, block.shape[dim] - width, None, axis...  8.98 us
    dot_general x2, matrix products, apply_tiles(): jnp.einsum('otc,trc->otr', picked, tiles, preferred_element_type=jnp.floa...  8.18 us
    ppermute x2, starting transfers between devices, with_halo(): lax.ppermute(lax.slice_in_dim(block, 0, width, axis=dim), axis, backward)  3.84 us
    ppermute x2, waiting for transfers between devices, with_halo(): lax.ppermute(lax.slice_in_dim(block, 0, width, axis=dim), axis, backward)  3.59 us
  transfers between devices with their start and end apart: 4, of which 1 were waited for; matrix products, arithmetic and copies ran while one was open for 3% of the time, Pallas kernels for 0%

profile of v1, /device:TPU:25, one launch (start us, length us, event | category | flops | bytes accessed | tf_op | source)
XLA Modules:
  0.0 101.5 jit_solution(40808418700720760)
XLA Ops:
  0.0 0.7 fusion.30
  0.7 4.4 %collective-permute-start = (bf16[32,256]{1,0:T(8,128)(2,1)S(1)}, bf16[32,256]{1,0:T(8,128)(2,1)S(1)}, u32[]{:S(2)}, u32[]{:S(2)}) collective-permute-start(bf16[32,256]{1,0:T(8,128)(2,1)S(1)} %get-tuple-element.10), channel_id=1, source_target_pairs={{0,64},{64,128},{128,192},{192,256},{256,320},{320,384},{384,448},... | collective-permute-start | bytes 49160 | tf_op jit(solution)/shard_map/ppermute | solution.py:243
  5.2 1.9 %collective-permute-start.1 = (bf16[32,256]{1,0:T(8,128)(2,1)S(1)}, bf16[32,256]{1,0:T(8,128)(2,1)S(1)}, u32[]{:S(2)}, u32[]{:S(2)}) collective-permute-start(bf16[32,256]{1,0:T(8,128)(2,1)S(1)} %get-tuple-element.11), channel_id=1, source_target_pairs={{64,0},{128,64},{192,128},{256,192},{320,256},{384,320},{448,384},... | collective-permute-start | bytes 49160 | tf_op jit(solution)/shard_map/ppermute | solution.py:246
  7.1 0.7 compare_and_fusion
  7.8 1.4 %fusion.31 = (f32[1]{0:T(128)}, f32[1]{0:T(128)}, f32[1]{0:T(128)}) fusion(f32[3]{0:T(128)} %param.14), kind=kLoop, calls=%fused_computation.48 | loop fusion | bytes 24 | tf_op jit(solution)/shard_map/slice | solution.py:255
  9.2 0.7 convert_bitcast_fusion
  11.2 0.7 slice.39
  12.6 0.0 collective-permute-done
  12.6 0.0 collective-permute-done.1
  12.6 1.1 %copy_bitcast_fusion.1 = bf16[32,68,128]{2,0,1:T(8,128)(2,1)S(1)} fusion(bf16[32,256]{1,0:T(8,128)(2,1)S(1)} %collective-permute-done.1, bf16[32,8192]{1,0:T(8,128)(2,1)} %param.9, bf16[32,256]{1,0:T(8,128)(2,1)S(1)} %collective-permute-done), kind=kLoop, calls=%fused_computation.30 | loop fusion | flops 1671168 | bytes 1114112 | tf_op jit(solution)/shard_map/reshape | solution.py:275
  13.7 0.7 gather_fusion
  14.5 4.1 %convolution_bitcast_fusion.1 = f32[32,112,128]{2,0,1:T(8,128)S(1)} fusion(bf16[112,128,128]{2,1,0:T(8,128)(2,1)} %param.10, bf16[112,32,128]{2,1,0:T(8,128)(2,1)S(1)} %gather_fusion, pred[112]{0:T(512)(128)(4,1)S(1)} %get-tuple-element.6), kind=kOutput, calls=%fused_computation.3 | convolution fusion | flops 117899264 | bytes 6422640 | tf_op jit(solution)/shard_map/otc,trc->otr/dot_general | solution.py:277
  18.6 0.0 copy-start.1
  18.6 0.1 slice.53
  18.7 0.9 fusion.18
  19.6 0.1 copy-done.1
  19.6 0.7 fusion.3
  20.4 4.6 %collective-permute-start.2 = (bf16[32,256]{1,0:T(8,128)(2,1)S(1)}, bf16[32,256]{1,0:T(8,128)(2,1)S(1)}, u32[]{:S(2)}, u32[]{:S(2)}) collective-permute-start(bf16[32,256]{1,0:T(8,128)(2,1)S(1)} %get-tuple-element.8), channel_id=1, source_target_pairs={{0,64},{64,128},{128,192},{192,256},{256,320},{320,384},{384,448},... | collective-permute-start | bytes 49160 | tf_op jit(solution)/shard_map/ppermute | solution.py:243
  25.0 1.9 %collective-permute-start.3 = (bf16[32,256]{1,0:T(8,128)(2,1)S(1)}, bf16[32,256]{1,0:T(8,128)(2,1)S(1)}, u32[]{:S(2)}, u32[]{:S(2)}) collective-permute-start(bf16[32,256]{1,0:T(8,128)(2,1)S(1)} %get-tuple-element.9), channel_id=1, source_target_pairs={{64,0},{128,64},{192,128},{256,192},{320,256},{384,320},{448,384},... | collective-permute-start | bytes 49160 | tf_op jit(solution)/shard_map/ppermute | solution.py:246
  27.1 0.0 collective-permute-done.2
  27.1 3.6 %collective-permute-done.3 = bf16[32,256]{1,0:T(8,128)(2,1)S(1)} collective-permute-done((bf16[32,256]{1,0:T(8,128)(2,1)S(1)}, bf16[32,256]{1,0:T(8,128)(2,1)S(1)}, u32[]{:S(2)}, u32[]{:S(2)}) %collective-permute-start.3) | collective-permute-done | bytes 16416 | tf_op jit(solution)/shard_map/ppermute | solution.py:246
  30.7 0.1 copy_bitcast_fusion
  30.8 0.7 gather_fusion.1
  31.5 4.1 %convolution_bitcast_fusion = f32[32,112,128]{2,0,1:T(8,128)S(1)} fusion(bf16[112,128,128]{2,1,0:T(8,128)(2,1)} %param.10, bf16[112,32,128]{2,1,0:T(8,128)(2,1)S(1)} %gather_fusion.1, pred[112]{0:T(512)(128)(4,1)S(1)} %get-tuple-element.6), kind=kOutput, calls=%fused_computation.2 | convolution fusion | flops 117899264 | bytes 6422640 | tf_op jit(solution)/shard_map/otc,trc->otr/dot_general | solution.py:277
  35.6 0.1 slice.57
  35.7 0.9 fusion.16
  36.6 0.0 copy-start
  36.6 0.8 fusion.6.f2_hbm
  37.4 0.1 copy-done
  37.5 63.2 %shard_map.73 = bf16[32,8192]{1,0:T(8,128)(2,1)S(1)} custom-call(bf16[32,8192]{1,0:T(8,128)(2,1)S(1)} %fusion.6.f2_hbm, bf16[32,2048]{1,0:T(8,128)(2,1)S(1)} %copy-done), custom_call_target="tpu_custom_call" | custom-call | tf_op jit(solution)/shard_map/pallas_call | solution.py:216
  100.7 0.8 copy.39
  (2 shorter events, 0.0 us)
Async XLA Ops:
  0.7 11.8 %collective-permute-start = (bf16[32,256]{1,0:T(8,128)(2,1)S(1)}, bf16[32,256]{1,0:T(8,128)(2,1)S(1)}, u32[]{:S(2)}, u32[]{:S(2)}) collective-permute-start(bf16[32,256]{1,0:T(8,128)(2,1)S(1)} %get-tuple-element.10), channel_id=1, source_target_pairs={{0,64},{64,128},{128,192},{192,256},{256,320},{320,384},{384,448},... | collective-permute-start | bytes 49160 | tf_op jit(solution)/shard_map/ppermute | solution.py:243
  5.2 7.4 %collective-permute-start.1 = (bf16[32,256]{1,0:T(8,128)(2,1)S(1)}, bf16[32,256]{1,0:T(8,128)(2,1)S(1)}, u32[]{:S(2)}, u32[]{:S(2)}) collective-permute-start(bf16[32,256]{1,0:T(8,128)(2,1)S(1)} %get-tuple-element.11), channel_id=1, source_target_pairs={{64,0},{128,64},{192,128},{256,192},{320,256},{384,320},{448,384},... | collective-permute-start | bytes 49160 | tf_op jit(solution)/shard_map/ppermute | solution.py:246
  18.6 1.1 %copy-start.1 = (bf16[32,8192]{1,0:T(8,128)(2,1)S(1)}, bf16[32,8192]{1,0:T(8,128)(2,1)}, u32[]{:S(2)}) copy-start(bf16[32,8192]{1,0:T(8,128)(2,1)} %param.9) | copy-start | bytes 1572868
  20.4 6.7 %collective-permute-start.2 = (bf16[32,256]{1,0:T(8,128)(2,1)S(1)}, bf16[32,256]{1,0:T(8,128)(2,1)S(1)}, u32[]{:S(2)}, u32[]{:S(2)}) collective-permute-start(bf16[32,256]{1,0:T(8,128)(2,1)S(1)} %get-tuple-element.8), channel_id=1, source_target_pairs={{0,64},{64,128},{128,192},{192,256},{256,320},{320,384},{384,448},... | collective-permute-start | bytes 49160 | tf_op jit(solution)/shard_map/ppermute | solution.py:243
  25.0 5.7 %collective-permute-start.3 = (bf16[32,256]{1,0:T(8,128)(2,1)S(1)}, bf16[32,256]{1,0:T(8,128)(2,1)S(1)}, u32[]{:S(2)}, u32[]{:S(2)}) collective-permute-start(bf16[32,256]{1,0:T(8,128)(2,1)S(1)} %get-tuple-element.9), channel_id=1, source_target_pairs={{64,0},{128,64},{192,128},{256,192},{320,256},{384,320},{448,384},... | collective-permute-start | bytes 49160 | tf_op jit(solution)/shard_map/ppermute | solution.py:246
  36.6 0.9 copy-start

commit v2 on v0

v2 whole, which is shorter than its diff:
```python
import jax
import jax.numpy as jnp
from jax import lax
from jax.experimental import pallas as pl
from jax.experimental.pallas import tpu as pltpu
from jax.sharding import PartitionSpec as P

HB = 2
NX, NZ = 4, 8
CHIPS = NX * NZ
N_SLAB = 8
N_ORB = 2 * CHIPS
NORB_DEV = 32
TILE = 128
PAIR = 2 * TILE
BLOCKS = 64
EXTRA = 48
COL, WHICH, GOES_ON, LAST, LIVE, ENTRIES = 0, 48, 96, 144, 208, 272
ROWS_DEV = BLOCKS * TILE
STEPS = 4
UNROLL = 8
MESH = pl.DeviceIdType.MESH
BF16, F32 = jnp.bfloat16, jnp.float32


def column_group(core, half, step, z):
    owner_x = 2 * core + lax.rem(step + z, 2)
    z_pair = half + 2 * lax.rem(step // 2 + z // 2, 2)
    return owner_x * 4 + z_pair


def aligned(index, size):
    return pl.ds(pl.multiple_of(index * size, size), size)


def kernel(
    table_hbm, bounds_hbm, orb_hbm, tiles_hbm, r_hbm, out_hbm,
    table, bounds, e0, e1, diag, extra, acc, seg, coef, f2, rv, rb, fb, ft, ob, ov,
    in_sem, h_send, h_recv, z_send, z_recv, x_send, x_recv,
    f_send, f_recv, g_send, g_recv, o_send, o_recv, out_sem,
):
    s, o = lax.axis_index("slab"), lax.axis_index("orb")
    core, chip = lax.rem(o, 2), o // 2
    z, x = lax.rem(chip, NZ), chip // NZ
    half = lax.rem(s, 2)
    partner = o + 1 - 2 * core
    x_up, x_down = lax.rem(x + 1, NX), lax.rem(x + NX - 1, NX)
    x_far = lax.rem(x + 2, NX)
    s_up, s_down = lax.rem(s + 1, N_SLAB), lax.rem(s + N_SLAB - 1, N_SLAB)
    not_first, not_last = s > 0, s < N_SLAB - 1

    loads = [
        pltpu.make_async_copy(table_hbm, table, in_sem.at[0]),
        pltpu.make_async_copy(bounds_hbm, bounds, in_sem.at[4]),
        pltpu.make_async_copy(r_hbm, rv, in_sem.at[1]),
        pltpu.make_async_copy(tiles_hbm.at[pl.ds(0, BLOCKS)], diag, in_sem.at[2]),
        pltpu.make_async_copy(tiles_hbm.at[pl.ds(BLOCKS, EXTRA)], extra, in_sem.at[3]),
    ]
    for load in loads:
        load.start()

    def load_block(b, carry):
        pltpu.make_async_copy(orb_hbm.at[:, aligned(b, TILE)], e0.at[HB + b], in_sem.at[5]).start()
        return carry

    lax.fori_loop(0, BLOCKS, load_block, 0)

    def wait_bytes(ref, sem):
        pltpu.make_async_copy(ref, ref, sem).wait()

    barrier = pltpu.get_barrier_semaphore()

    def greet(i, carry):
        there = lax.rem(o + i, N_ORB)

        @pl.when(i > 0)
        def _():
            pl.semaphore_signal(barrier, inc=1, device_id=(s, there), device_id_type=MESH)

        for other in (s_up, s_down):
            pl.semaphore_signal(barrier, inc=1, device_id=(other, there), device_id_type=MESH)
        return carry

    lax.fori_loop(0, N_ORB, greet, 0)

    loads[0].wait()
    loads[1].wait()
    lower = jnp.full((8, TILE), bounds[0]) - 3.0
    cutoff = jnp.full((8, TILE), bounds[1]) - 0.5
    upper = jnp.full((8, TILE), bounds[2]) + 3.0
    half_width = (upper - cutoff) / 2.0
    center = (upper + cutoff) / 2.0
    sigma_one = half_width / (lower - center)
    sigma_two = 1.0 / (2.0 / sigma_one - sigma_one)
    coef[0] = center
    coef[1] = sigma_one / half_width
    coef[2] = 2.0 * sigma_two / half_width
    coef[3] = sigma_one * sigma_two

    for ext in (e0, e1):
        @pl.when(s == 0)
        def _():
            ext[:HB] = jnp.zeros((HB, NORB_DEV, TILE), BF16)

        @pl.when(s == N_SLAB - 1)
        def _():
            ext[HB + BLOCKS:] = jnp.zeros((HB, NORB_DEV, TILE), BF16)

    seg[EXTRA] = jnp.zeros((NORB_DEV, TILE), F32)

    loads[2].wait()
    wait_bytes(e0.at[pl.ds(HB, BLOCKS)], in_sem.at[5])
    pl.semaphore_wait(barrier, 3 * N_ORB - 1)

    def send(src, dst, send_sem, recv_sem, to):
        pltpu.make_async_remote_copy(
            src_ref=src, dst_ref=dst, send_sem=send_sem, recv_sem=recv_sem,
            device_id=to, device_id_type=MESH,
        ).start()

    low_edge, high_edge = pl.ds(0, HB), pl.ds(HB + BLOCKS, HB)

    def send_edges(ext, which):
        @pl.when(not_last)
        def _():
            send(ext.at[pl.ds(BLOCKS, HB)], ext.at[low_edge],
                 h_send.at[which, 0], h_recv.at[which, 0], (s_up, o))

        @pl.when(not_first)
        def _():
            send(ext.at[pl.ds(HB, HB)], ext.at[high_edge],
                 h_send.at[which, 1], h_recv.at[which, 1], (s_down, o))

    def wait_edges(ext, which):
        @pl.when(not_first)
        def _():
            wait_bytes(ext.at[low_edge], h_recv.at[which, 0])

        @pl.when(not_last)
        def _():
            wait_bytes(ext.at[high_edge], h_recv.at[which, 1])

    send_edges(e0, 0)

    def rotation_columns(to_core, step, to_z):
        return rv.at[:, aligned(column_group(to_core, half, step, to_z), TILE)]

    def z_step(step, carry):
        pltpu.make_async_copy(
            rotation_columns(core, step, z), rb.at[step, core, chip], z_recv.at[step]
        ).start()

        def one(i, inner):
            there = lax.rem(z * 2 + core + i, 2 * NZ)
            send(
                rotation_columns(lax.rem(there, 2), step, there // 2),
                rb.at[step, core, chip], z_send, z_recv.at[step], (s, x * 2 * NZ + there),
            )
            return inner

        lax.fori_loop(1, 2 * NZ, one, 0)
        return carry

    lax.fori_loop(0, STEPS, z_step, 0)

    def of_x(step, at_x):
        return rb.at[step, :, pl.ds(at_x * NZ, NZ)]

    def of_x_core(step, at_core, at_x):
        return rb.at[step, at_core, pl.ds(at_x * NZ, NZ)]

    def orb_at(at_x):
        return (at_x * NZ + z) * 2 + core

    def stage_one(step):
        mine = of_x(step, x)
        wait_bytes(mine, z_recv.at[step])
        send(mine, mine, x_send, x_recv.at[step, 0], (s, orb_at(x_up)))
        send(mine, mine, x_send, x_recv.at[step, 1], (s, orb_at(x_down)))

    def stage_two(step):
        wait_bytes(of_x(step, x_down), x_recv.at[step, 0])
        relayed = of_x_core(step, 0, x_down)
        send(relayed, relayed, x_send, x_recv.at[step, 2], (s, orb_at(x_up)))
        wait_bytes(of_x(step, x_up), x_recv.at[step, 1])
        relayed = of_x_core(step, 1, x_up)
        send(relayed, relayed, x_send, x_recv.at[step, 3], (s, orb_at(x_down)))

    def stage_three(step):
        wait_bytes(of_x_core(step, 0, x_far), x_recv.at[step, 2])
        wait_bytes(of_x_core(step, 1, x_far), x_recv.at[step, 3])

    def times_tile(rows, tile):
        return lax.dot_general(rows, tile, (((1,), (1,)), ((), ())), preferred_element_type=F32)

    def apply_diagonal(ext):
        def body(i, carry):
            for u in range(UNROLL):
                b = i * UNROLL + u
                acc[b] = times_tile(ext[b + HB], diag[b])
            return carry

        lax.fori_loop(0, BLOCKS // UNROLL, body, 0)

    def apply_extra(ext):
        def multiply(i, carry):
            for u in range(UNROLL):
                m = i * UNROLL + u
                seg[m] = times_tile(ext[table[COL + m]], extra[table[WHICH + m]])
            return carry

        lax.fori_loop(0, EXTRA // UNROLL, multiply, 0)

        def add_up(i, run):
            for u in range(UNROLL):
                m = i * UNROLL + u
                run = seg[m] + table[GOES_ON + m].astype(F32) * run
                seg[m] = run
            return run

        lax.fori_loop(0, EXTRA // UNROLL, add_up, jnp.zeros((NORB_DEV, TILE), F32))

    lanes = lax.broadcasted_iota(jnp.int32, (1, TILE), 1)

    def filtered_first(b):
        total = acc[b] + seg[table[LAST + b]]
        source = e0[b + HB].astype(F32)
        value = (total - coef[0, 0:1] * source) * coef[1, 0:1]
        e1[b + HB] = jnp.where(lanes < table[LIVE + b], value, 0.0).astype(BF16)

    def filtered_second(b):
        total = acc[b] + seg[table[LAST + b]]
        source = e0[b + HB].astype(F32)
        first = e1[b + HB].astype(F32)
        value = (total - coef[0, 0:1] * first) * coef[2, 0:1] - coef[3, 0:1] * source
        return jnp.where(lanes < table[LIVE + b], value, 0.0).astype(BF16)

    loads[3].wait()
    apply_diagonal(e0)
    loads[4].wait()
    wait_edges(e0, 0)
    apply_extra(e0)
    for b in (0, 1, BLOCKS - 2, BLOCKS - 1):
        filtered_first(b)
    send_edges(e1, 1)

    def inner_first(i, carry):
        for u in range(4):
            filtered_first(HB + 4 * i + u)
        return carry

    lax.fori_loop(0, (BLOCKS - 2 * HB) // 4, inner_first, 0)
    apply_diagonal(e1)
    stage_one(0)
    wait_edges(e1, 1)
    apply_extra(e1)
    stage_one(1)

    def destination(i):
        return lax.rem(x + i // NZ, NX) * NZ + lax.rem(z + lax.rem(i, NZ), NZ)

    def f_one(i, carry):
        there = destination(i)
        f2[there, :, :TILE] = filtered_second(2 * there)
        f2[there, :, TILE:] = filtered_second(2 * there + 1)

        @pl.when(i > 0)
        def _():
            send(f2.at[there], fb.at[core, chip, :, pl.ds(0, PAIR)], f_send, f_recv.at[x], (s, there * 2 + core))

        @pl.when(i == 0)
        def _():
            pltpu.make_async_copy(f2.at[there], fb.at[core, chip, :, pl.ds(0, PAIR)], f_recv.at[x]).start()

        return carry

    lax.fori_loop(0, CHIPS, f_one, 0)

    def turn(at_core, at_x, first_row):
        for group in range(2):
            block = fb[at_core, pl.ds(at_x * NZ + 4 * group, 4), :, first_row:first_row + TILE]
            k = at_core * (CHIPS * NORB_DEV) + (at_x * 2 + group) * TILE
            ft[first_row:first_row + TILE, aligned(k // TILE, TILE)] = block.reshape(TILE, TILE).T

    def pass_on(at_x):
        at = pl.ds(at_x * NZ, NZ)
        got = fb.at[core, at, :, pl.ds(0, PAIR)]
        wait_bytes(got, f_recv.at[at_x])
        for to in (o, partner):
            send(fb.at[core, at, :, pl.ds(0, TILE)], fb.at[core, at, :, pl.ds(PAIR, TILE)],
                 g_send, g_recv.at[at_x, 1], (s_up, to))
            send(fb.at[core, at, :, pl.ds(TILE, TILE)], fb.at[core, at, :, pl.ds(PAIR + TILE, TILE)],
                 g_send, g_recv.at[at_x, 2], (s_down, to))
        send(got, got, g_send, g_recv.at[at_x, 0], (s, partner))
        turn(core, at_x, 0)
        turn(core, at_x, TILE)

    def take(at_x):
        at = pl.ds(at_x * NZ, NZ)
        wait_bytes(fb.at[1 - core, at, :, pl.ds(0, PAIR)], g_recv.at[at_x, 0])
        turn(1 - core, at_x, 0)
        turn(1 - core, at_x, TILE)
        for side in range(2):
            wait_bytes(fb.at[:, at, :, pl.ds(PAIR + side * TILE, TILE)], g_recv.at[at_x, 1 + side])
            turn(0, at_x, PAIR + side * TILE)
            turn(1, at_x, PAIR + side * TILE)

    def back_x(i):
        return lax.rem(x + NX - i, NX)

    stage_one(2)
    stage_one(3)
    stage_two(0)
    stage_two(1)
    pass_on(back_x(0))
    stage_three(0)
    stage_two(2)
    pass_on(back_x(1))
    stage_three(1)
    stage_two(3)
    pass_on(back_x(2))
    stage_three(2)
    pass_on(back_x(3))
    for i in range(NX):
        take(back_x(i))
    stage_three(3)

    def rotate(step, carry):
        slot = rb[step].reshape(2 * CHIPS * NORB_DEV, TILE)
        made = jnp.dot(ft[...], slot, preferred_element_type=F32)
        ob[step] = made.T.astype(BF16)
        first = column_group(core, half, step, z) * 4
        own = pl.ds(pl.multiple_of(chip * PAIR, PAIR), PAIR)
        low = pl.ds(pl.multiple_of(chip * PAIR, TILE), TILE)
        high = pl.ds(pl.multiple_of(chip * PAIR + TILE, TILE), TILE)
        for i in range(4):
            rows = pl.ds(i * NORB_DEV, NORB_DEV)
            owner = first + i
            send(ob.at[step, rows, pl.ds(PAIR, TILE)], ov.at[:, low], o_send, o_recv, (s_down, owner))
            send(ob.at[step, rows, pl.ds(PAIR + TILE, TILE)], ov.at[:, high], o_send, o_recv, (s_up, owner))
            piece = ob.at[step, rows, pl.ds(0, PAIR)]

            @pl.when(owner == o)
            def _():
                pltpu.make_async_copy(piece, ov.at[:, own], o_recv).start()

            @pl.when(owner != o)
            def _():
                send(piece, ov.at[:, own], o_send, o_recv, (s, owner))

        return carry

    lax.fori_loop(0, STEPS, rotate, 0)

    wait_bytes(ov, o_recv)
    store = pltpu.make_async_copy(ov, out_hbm, out_sem)
    store.start()
    for which, ext in ((0, e0), (1, e1)):
        @pl.when(not_last)
        def _():
            wait_bytes(ext.at[low_edge], h_send.at[which, 0])

        @pl.when(not_first)
        def _():
            wait_bytes(ext.at[high_edge], h_send.at[which, 1])

    wait_bytes(rb.at[0, :, pl.ds(0, 30)], z_send)
    wait_bytes(rb.at[pl.ds(0, 3)], x_send)
    wait_bytes(f2.at[pl.ds(0, CHIPS - 1)], f_send)
    wait_bytes(fb.at[:, :, :, pl.ds(0, PAIR + TILE)], g_send)
    mine_too = (x // 2 == core) & (lax.rem(z // 2, 2) == half)

    @pl.when(mine_too)
    def _():
        wait_bytes(f2.at[pl.ds(0, CHIPS - 1)], o_send)

    @pl.when(jnp.logical_not(mine_too))
    def _():
        wait_bytes(f2, o_send)

    store.wait()


def small_table(tile_rows, tile_cols, row_counts):
    rows, cols = tile_rows[BLOCKS:], tile_cols[BLOCKS:] + HB
    count = jnp.arange(EXTRA, dtype=jnp.int32)
    same_before = (rows[None, :] == rows[:, None]) & (count[None, :] < count[:, None])
    place = jnp.sum(((rows[None, :] < rows[:, None]) | same_before).astype(jnp.int32), axis=1)
    goes_on = jnp.max(same_before.astype(jnp.int32), axis=1)
    def in_order(values):
        return jnp.sum(jnp.where(place[None, :] == count[:, None], values[None, :], 0), axis=1)

    block = jnp.arange(BLOCKS, dtype=jnp.int32)
    up_to = jnp.sum((rows[None, :] <= block[:, None]).astype(jnp.int32), axis=1)
    any_tile = jnp.any(rows[None, :] == block[:, None], axis=1)
    return jnp.concatenate([in_order(cols), in_order(count), in_order(goes_on), jnp.where(any_tile, up_to - 1, EXTRA), row_counts])


def local(orbitals_t, tiles, tile_rows, tile_cols, row_counts, bounds, rotation):
    dma = pltpu.SemaphoreType.DMA
    ext = pltpu.VMEM((BLOCKS + 2 * HB, NORB_DEV, TILE), BF16)
    anywhere = pl.BlockSpec(memory_space=pl.ANY)
    return pl.pallas_call(
        kernel,
        out_shape=jax.ShapeDtypeStruct(orbitals_t.shape, BF16),
        in_specs=[anywhere] * 5,
        out_specs=anywhere,
        scratch_shapes=[
            pltpu.SMEM((ENTRIES,), jnp.int32),
            pltpu.SMEM((3,), F32),
            ext, ext,
            pltpu.VMEM((BLOCKS, TILE, TILE), BF16),
            pltpu.VMEM((EXTRA, TILE, TILE), BF16),
            pltpu.VMEM((BLOCKS, NORB_DEV, TILE), F32),
            pltpu.VMEM((EXTRA + 1, NORB_DEV, TILE), F32),
            pltpu.VMEM((4, 8, TILE), F32),
            pltpu.VMEM((CHIPS, NORB_DEV, PAIR), BF16),
            pltpu.VMEM((NORB_DEV, N_ORB * NORB_DEV), BF16),
            pltpu.VMEM((STEPS, 2, CHIPS, NORB_DEV, TILE), BF16),
            pltpu.VMEM((2, CHIPS, NORB_DEV, 2 * PAIR), BF16),
            pltpu.VMEM((2 * PAIR, N_ORB * NORB_DEV), BF16),
            pltpu.VMEM((STEPS, TILE, 2 * PAIR), BF16),
            pltpu.VMEM((NORB_DEV, ROWS_DEV), BF16),
            dma((6,)), dma((2, 2)), dma((2, 2)), dma, dma((STEPS,)), dma, dma((STEPS, 4)),
            dma, dma((NX,)), dma, dma((NX, 3)), dma, dma, dma,
        ],
        compiler_params=pltpu.CompilerParams(
            collective_id=0, has_side_effects=True, vmem_limit_bytes=40 << 20
        ),
    )(small_table(tile_rows, tile_cols, row_counts), bounds, orbitals_t, tiles, rotation)


def solution(mesh):
    return jax.shard_map(
        local,
        mesh=mesh,
        in_specs=(
            P("orb", "slab"),
            P("slab", None, None),
            P("slab"),
            P("slab"),
            P("slab"),
            P(),
            P("orb", None),
        ),
        out_specs=P("orb", "slab"),
        check_vma=False,
    )
```

time: 142 us -> 85 us (0.60)
  Pallas kernels: 0 us -> 76.6 us
  blocking collectives: 55.4 us -> 0 us
  waiting for transfers between devices: 35.1 us -> 0 us
  between operations: 15.6 us -> 0.02 us
  matrix products: 14.7 us -> 0 us
  starting transfers between devices: 10.6 us -> 0 us
  other arithmetic: 4.15 us -> 1.26 us
    pallas_call x0 -> x1, Pallas kernels: none -> 76.6 us  [local(): pl.pallas_call(kernel, out_shape=jax.ShapeDtypeStruct(orbitals_t.shape, B...]
    all_to_all x2 -> x0, blocking collectives: 55.4 us -> none  [the longest x1 32.7 us: local(): lax.all_to_all(filtered_two, 'orb', split_axis=1, concat_axis=0, tiled=True)]
    all_gather x1 -> x0, waiting for transfers between devices: 30.9 us -> none  [local(): lax.all_gather(rotation, 'orb', axis=0, tiled=True)]
    dot_general x5 -> x0, matrix products: 14.7 us -> none  [the longest x2 8.23 us: apply_tiles(): jnp.einsum('otc,trc->otr', picked, tiles, preferred_element_type=jnp.floa...]
    ppermute x4 -> x0, starting transfers between devices: 10.6 us -> none  [the longest x2 7.99 us: with_halo(): lax.ppermute(lax.slice_in_dim(block, block.shape[dim] - width, None, axis...]
    unnamed x2 -> x9, local copies, waits for them, and re-layouts: 0.09 us -> 5.44 us
    ppermute x4 -> x0, waiting for transfers between devices: 3.41 us -> none  [the longest x2 3.41 us: with_halo(): lax.ppermute(lax.slice_in_dim(block, 0, width, axis=dim), axis, backward)]
    slice x6 -> x1, local copies, waits for them, and re-layouts: 3.02 us -> 0.73 us  [small_table(): rows, cols = (tile_rows[BLOCKS:], tile_cols[BLOCKS:] + HB)]
  transfers between devices with their start and end apart: 5 -> 0, of which waited for: 2 -> 0; matrix products, arithmetic and copies ran while one was open for 13% -> 0% of each run, Pallas kernels for 0% -> 0%
where the time goes in v2:
time: 85 us; the launch traced here: 84.8 us
  Pallas kernels  76.6 us (90%)
  local copies, waits for them, and re-layouts  6.9 us (8%)
  other arithmetic  1.26 us (1%)
    pallas_call x1, Pallas kernels, local(): pl.pallas_call(kernel, out_shape=jax.ShapeDtypeStruct(orbitals_t.shape, B...  76.6 us
    unnamed x9, local copies, waits for them, and re-layouts  5.44 us

profile of v2, /device:TPU:1, one launch (start us, length us, event | category | flops | bytes accessed | tf_op | source)
XLA Modules:
  0.0 84.8 jit_solution(15743268118413400643)
XLA Ops:
  0.0 0.7 slice.6
  0.7 0.1 fusion.1
  0.8 0.1 convert_reduce_fusion
  0.9 0.7 slice_add_fusion
  1.7 0.2 convert_reduce_fusion.1
  1.8 0.2 select_reduce_fusion
  2.0 0.7 concatenate.3.table_hbm
  2.7 0.0 copy-start
  2.7 2.0 %copy-done = bf16[112,128,128]{2,1,0:T(8,128)(2,1)S(1)} copy-done((bf16[112,128,128]{2,1,0:T(8,128)(2,1)S(1)}, bf16[112,128,128]{2,1,0:T(8,128)(2,1)}, u32[]{:S(2)}) %copy-start) | copy-done | bytes 3670040
  4.8 0.0 copy-start.1
  4.8 1.0 %copy-done.1 = bf16[32,8192]{1,0:T(8,128)(2,1)S(1)} copy-done((bf16[32,8192]{1,0:T(8,128)(2,1)S(1)}, bf16[32,8192]{1,0:T(8,128)(2,1)}, u32[]{:S(2)}) %copy-start.1) | copy-done | bytes 524312
  5.8 0.0 copy-start.2
  5.8 0.9 %copy-done.2 = bf16[32,2048]{1,0:T(8,128)(2,1)S(1)} copy-done((bf16[32,2048]{1,0:T(8,128)(2,1)S(1)}, bf16[32,2048]{1,0:T(8,128)(2,1)}, u32[]{:S(2)}) %copy-start.2) | copy-done | bytes 131096
  6.7 0.0 copy-start.3
  6.7 0.7 copy-done.3
  7.4 76.6 %shard_map.73 = bf16[32,8192]{1,0:T(8,128)(2,1)S(1)} custom-call(s32[272]{0:T(512)S(1)} %concatenate.3.table_hbm, f32[3]{0:T(128)S(1)} %copy-done.3, bf16[32,8192]{1,0:T(8,128)(2,1)S(1)} %copy-done.1, bf16[112,128,128]{2,1,0:T(8,128)(2,1)S(1)} %copy-done, bf16[32,2048]{1,0:T(8,128)(2,1)S(1)} %copy-done.2), custom_call_target="tpu_custom_call" | custom-call | tf_op jit(solution)/shard_map/pallas_call | solution.py:403
  84.0 0.8 copy.9
  (1 shorter events, 0.0 us)
Async XLA Ops:
  2.7 2.0 %copy-start = (bf16[112,128,128]{2,1,0:T(8,128)(2,1)S(1)}, bf16[112,128,128]{2,1,0:T(8,128)(2,1)}, u32[]{:S(2)}) copy-start(bf16[112,128,128]{2,1,0:T(8,128)(2,1)} %tiles_hbm.1) | copy-start | bytes 11010052
  4.8 1.0 %copy-start.1 = (bf16[32,8192]{1,0:T(8,128)(2,1)S(1)}, bf16[32,8192]{1,0:T(8,128)(2,1)}, u32[]{:S(2)}) copy-start(bf16[32,8192]{1,0:T(8,128)(2,1)} %orb_hbm.1) | copy-start | bytes 1572868
  5.8 0.9 %copy-start.2 = (bf16[32,2048]{1,0:T(8,128)(2,1)S(1)}, bf16[32,2048]{1,0:T(8,128)(2,1)}, u32[]{:S(2)}) copy-start(bf16[32,2048]{1,0:T(8,128)(2,1)} %r_hbm.1) | copy-start | bytes 393220
  6.7 0.7 copy-start.3

commit v3 on v2

--- a/solution.py
+++ b/solution.py
@@ -15,7 +15,7 @@
 PAIR = 2 * TILE
 BLOCKS = 64
 EXTRA = 48
-COL, WHICH, GOES_ON, LAST, LIVE, ENTRIES = 0, 48, 96, 144, 208, 272
+TILES = BLOCKS + EXTRA
 ROWS_DEV = BLOCKS * TILE
 STEPS = 4
 UNROLL = 8
@@ -34,9 +34,9 @@
 
 
 def kernel(
-    table_hbm, bounds_hbm, orb_hbm, tiles_hbm, r_hbm, out_hbm,
-    table, bounds, e0, e1, diag, extra, acc, seg, coef, f2, rv, rb, fb, ft, ob, ov,
-    in_sem, h_send, h_recv, z_send, z_recv, x_send, x_recv,
+    rows_hbm, cols_hbm, counts_hbm, bounds_hbm, orb_hbm, tiles_hbm, r_hbm, out_hbm,
+    t_rows, t_cols, t_made, col_at, which_at, goes_on_at, last_at, counts, bounds, e0, e1, diag, extra, acc, seg, coef, f2, rv, rb, fb, ft, ob, ov,
+    in_sem, t_sem, h_send, h_recv, z_send, z_recv, x_send, x_recv,
     f_send, f_recv, g_send, g_recv, o_send, o_recv, out_sem,
 ):
     s, o = lax.axis_index("slab"), lax.axis_index("orb")
@@ -50,11 +50,13 @@
     not_first, not_last = s > 0, s < N_SLAB - 1
 
     loads = [
-        pltpu.make_async_copy(table_hbm, table, in_sem.at[0]),
+        pltpu.make_async_copy(rows_hbm, t_rows, in_sem.at[0]),
         pltpu.make_async_copy(bounds_hbm, bounds, in_sem.at[4]),
         pltpu.make_async_copy(r_hbm, rv, in_sem.at[1]),
         pltpu.make_async_copy(tiles_hbm.at[pl.ds(0, BLOCKS)], diag, in_sem.at[2]),
         pltpu.make_async_copy(tiles_hbm.at[pl.ds(BLOCKS, EXTRA)], extra, in_sem.at[3]),
+        pltpu.make_async_copy(cols_hbm, t_cols, in_sem.at[6]),
+        pltpu.make_async_copy(counts_hbm, counts, in_sem.at[7]),
     ]
     for load in loads:
         load.start()
@@ -70,20 +72,36 @@
 
     barrier = pltpu.get_barrier_semaphore()
 
-    def greet(i, carry):
-        there = lax.rem(o + i, N_ORB)
-
-        @pl.when(i > 0)
-        def _():
-            pl.semaphore_signal(barrier, inc=1, device_id=(s, there), device_id_type=MESH)
-
-        for other in (s_up, s_down):
-            pl.semaphore_signal(barrier, inc=1, device_id=(other, there), device_id_type=MESH)
-        return carry
-
-    lax.fori_loop(0, N_ORB, greet, 0)
-
-    loads[0].wait()
+    same_parity = lax.rem(z // 2, 2) == half
+
+    def signal(to):
+        pl.semaphore_signal(barrier, inc=1, device_id=to, device_id_type=MESH)
+
+    def greet_chip(i, carry):
+        signal((s, lax.rem(chip + i, CHIPS) * 2 + core))
+        return carry
+
+    def greet_column(i, carry):
+        signal((s, (x * NZ + i) * 2 + 1 - core))
+        return carry
+
+    def greet_other(i, carry):
+        signal((s, lax.rem(chip + i, CHIPS) * 2 + 1 - core))
+        return carry
+
+    def greet_near(i, carry):
+        for near in (s_up, s_down):
+            signal((near, lax.rem(chip + i, CHIPS) * 2 + x // 2))
+        return carry
+
+    for near in (s_up, s_down):
+        for to in (o, partner):
+            signal((near, to))
+    lax.fori_loop(1, CHIPS, greet_chip, 0)
+    lax.fori_loop(0, NZ, greet_column, 0)
+    lax.fori_loop(0, jnp.where(same_parity & (core != x // 2), CHIPS, 0), greet_other, 0)
+    lax.fori_loop(0, jnp.where(same_parity, 0, CHIPS), greet_near, 0)
+
     loads[1].wait()
     lower = jnp.full((8, TILE), bounds[0]) - 3.0
     cutoff = jnp.full((8, TILE), bounds[1]) - 0.5
@@ -110,7 +128,7 @@
 
     loads[2].wait()
     wait_bytes(e0.at[pl.ds(HB, BLOCKS)], in_sem.at[5])
-    pl.semaphore_wait(barrier, 3 * N_ORB - 1)
+    pl.semaphore_wait(barrier, 4 + (CHIPS - 1) + NZ + 8 + 32)
 
     def send(src, dst, send_sem, recv_sem, to):
         pltpu.make_async_remote_copy(
@@ -190,6 +208,38 @@
         wait_bytes(of_x_core(step, 0, x_far), x_recv.at[step, 2])
         wait_bytes(of_x_core(step, 1, x_far), x_recv.at[step, 3])
 
+    table_copies = [
+        pltpu.make_async_copy(t_made.at[pl.ds(i, 1)], to, t_sem.at[i])
+        for i, to in enumerate((col_at, which_at, goes_on_at, last_at))
+    ]
+
+    def make_table():
+        listed = (TILES, TILES)
+        down = lax.broadcasted_iota(jnp.int32, listed, 0)
+        along = lax.broadcasted_iota(jnp.int32, listed, 1)
+        row_along = jnp.broadcast_to(t_rows[...], listed)
+        col_along = jnp.broadcast_to(t_cols[...] + HB, listed)
+        row_down = jnp.sum(jnp.where(down == along, row_along, 0), axis=1, keepdims=True)
+        col_down = jnp.sum(jnp.where(down == along, col_along, 0), axis=1, keepdims=True)
+        same_before = (row_along == row_down) & (along < down) & (along >= BLOCKS)
+        before = same_before | ((row_along < row_down) & (along >= BLOCKS))
+        place = jnp.sum(jnp.where(before, 1, 0), axis=1, keepdims=True)
+        goes_on = jnp.minimum(jnp.sum(jnp.where(same_before, 1, 0), axis=1, keepdims=True), 1)
+        here = (place == along) & (down >= BLOCKS)
+
+        def in_order(values):
+            return jnp.sum(jnp.where(here, values, 0), axis=0, keepdims=True)
+
+        is_extra = down >= BLOCKS
+        up_to = jnp.sum(jnp.where(is_extra & (row_down <= along), 1, 0), axis=0, keepdims=True)
+        below = jnp.sum(jnp.where(is_extra & (row_down < along), 1, 0), axis=0, keepdims=True)
+        t_made[0:1] = in_order(col_down)
+        t_made[1:2] = in_order(down - BLOCKS)
+        t_made[2:3] = in_order(goes_on)
+        t_made[3:4] = jnp.where(up_to > below, up_to - 1, EXTRA)
+        for made in table_copies:
+            made.start()
+
     def times_tile(rows, tile):
         return lax.dot_general(rows, tile, (((1,), (1,)), ((), ())), preferred_element_type=F32)
 
@@ -206,7 +256,7 @@
         def multiply(i, carry):
             for u in range(UNROLL):
                 m = i * UNROLL + u
-                seg[m] = times_tile(ext[table[COL + m]], extra[table[WHICH + m]])
+                seg[m] = times_tile(ext[col_at[0, m]], extra[which_at[0, m]])
             return carry
 
         lax.fori_loop(0, EXTRA // UNROLL, multiply, 0)
@@ -214,7 +264,7 @@
         def add_up(i, run):
             for u in range(UNROLL):
                 m = i * UNROLL + u
-                run = seg[m] + table[GOES_ON + m].astype(F32) * run
+                run = seg[m] + goes_on_at[0, m].astype(F32) * run
                 seg[m] = run
             return run
 
@@ -223,21 +273,27 @@
     lanes = lax.broadcasted_iota(jnp.int32, (1, TILE), 1)
 
     def filtered_first(b):
-        total = acc[b] + seg[table[LAST + b]]
+        total = acc[b] + seg[last_at[0, b]]
         source = e0[b + HB].astype(F32)
         value = (total - coef[0, 0:1] * source) * coef[1, 0:1]
-        e1[b + HB] = jnp.where(lanes < table[LIVE + b], value, 0.0).astype(BF16)
+        e1[b + HB] = jnp.where(lanes < counts[b], value, 0.0).astype(BF16)
 
     def filtered_second(b):
-        total = acc[b] + seg[table[LAST + b]]
+        total = acc[b] + seg[last_at[0, b]]
         source = e0[b + HB].astype(F32)
         first = e1[b + HB].astype(F32)
         value = (total - coef[0, 0:1] * first) * coef[2, 0:1] - coef[3, 0:1] * source
-        return jnp.where(lanes < table[LIVE + b], value, 0.0).astype(BF16)
-
+        return jnp.where(lanes < counts[b], value, 0.0).astype(BF16)
+
+    loads[0].wait()
+    loads[5].wait()
+    make_table()
     loads[3].wait()
     apply_diagonal(e0)
     loads[4].wait()
+    for made in table_copies:
+        made.wait()
+    loads[6].wait()
     wait_edges(e0, 0)
     apply_extra(e0)
     for b in (0, 1, BLOCKS - 2, BLOCKS - 1):
@@ -381,21 +437,6 @@
     store.wait()
 
 
-def small_table(tile_rows, tile_cols, row_counts):
-    rows, cols = tile_rows[BLOCKS:], tile_cols[BLOCKS:] + HB
-    count = jnp.arange(EXTRA, dtype=jnp.int32)
-    same_before = (rows[None, :] == rows[:, None]) & (count[None, :] < count[:, None])
-    place = jnp.sum(((rows[None, :] < rows[:, None]) | same_before).astype(jnp.int32), axis=1)
-    goes_on = jnp.max(same_before.astype(jnp.int32), axis=1)
-    def in_order(values):
-        return jnp.sum(jnp.where(place[None, :] == count[:, None], values[None, :], 0), axis=1)
-
-    block = jnp.arange(BLOCKS, dtype=jnp.int32)
-    up_to = jnp.sum((rows[None, :] <= block[:, None]).astype(jnp.int32), axis=1)
-    any_tile = jnp.any(rows[None, :] == block[:, None], axis=1)
-    return jnp.concatenate([in_order(cols), in_order(count), in_order(goes_on), jnp.where(any_tile, up_to - 1, EXTRA), row_counts])
-
-
 def local(orbitals_t, tiles, tile_rows, tile_cols, row_counts, bounds, rotation):
     dma = pltpu.SemaphoreType.DMA
     ext = pltpu.VMEM((BLOCKS + 2 * HB, NORB_DEV, TILE), BF16)
@@ -403,10 +444,13 @@
     return pl.pallas_call(
         kernel,
         out_shape=jax.ShapeDtypeStruct(orbitals_t.shape, BF16),
-        in_specs=[anywhere] * 5,
+        in_specs=[anywhere] * 7,
         out_specs=anywhere,
         scratch_shapes=[
-            pltpu.SMEM((ENTRIES,), jnp.int32),
+            *[pltpu.VMEM((1, TILES), jnp.int32)] * 2,
+            pltpu.VMEM((8, TILES), jnp.int32),
+            *[pltpu.SMEM((1, TILES), jnp.int32)] * 4,
+            pltpu.SMEM((BLOCKS,), jnp.int32),
             pltpu.SMEM((3,), F32),
             ext, ext,
             pltpu.VMEM((BLOCKS, TILE, TILE), BF16),
@@ -421,13 +465,17 @@
             pltpu.VMEM((2 * PAIR, N_ORB * NORB_DEV), BF16),
             pltpu.VMEM((STEPS, TILE, 2 * PAIR), BF16),
             pltpu.VMEM((NORB_DEV, ROWS_DEV), BF16),
-            dma((6,)), dma((2, 2)), dma((2, 2)), dma, dma((STEPS,)), dma, dma((STEPS, 4)),
+            dma((8,)), dma((4,)), dma((2, 2)), dma((2, 2)), dma, dma((STEPS,)), dma, dma((STEPS, 4)),
             dma, dma((NX,)), dma, dma((NX, 3)), dma, dma, dma,
         ],
         compiler_params=pltpu.CompilerParams(
             collective_id=0, has_side_effects=True, vmem_limit_bytes=40 << 20
         ),
-    )(small_table(tile_rows, tile_cols, row_counts), bounds, orbitals_t, tiles, rotation)
+    )(
+        *(pltpu.with_memory_space_constraint(v, pltpu.HBM) for v in (
+            tile_rows.reshape(1, TILES), tile_cols.reshape(1, TILES), row_counts, bounds, orbitals_t, tiles, rotation,
+        ))
+    )
 
 
 def solution(mesh):

time: 85 us -> 77.5 us (0.912)
  local copies, waits for them, and re-layouts: 6.9 us -> 0.8 us
  other arithmetic: 1.26 us -> 0 us
    unnamed x9 -> x1, local copies, waits for them, and re-layouts: 5.44 us -> 0.8 us
where the time goes in v3:
time: 77.5 us; the launch traced here: 77.4 us
  Pallas kernels  76.6 us (99%)
  local copies, waits for them, and re-layouts  0.8 us (1%)
    pallas_call x1, Pallas kernels, local(): pl.pallas_call(kernel, out_shape=jax.ShapeDtypeStruct(orbitals_t.shape, B...  76.6 us

profile of v3, /device:TPU:1, one launch (start us, length us, event | category | flops | bytes accessed | tf_op | source)
XLA Modules:
  0.0 77.4 jit_solution(12185760729929807304)
XLA Ops:
  0.0 76.6 %shard_map.73 = bf16[32,8192]{1,0:T(8,128)(2,1)S(1)} custom-call(s32[1,112]{1,0:T(1,128)} %bitcast.2, s32[1,112]{1,0:T(1,128)} %bitcast.3, s32[64]{0:T(128)} %counts_hbm.1, f32[3]{0:T(128)} %bounds_hbm.1, bf16[32,8192]{1,0:T(8,128)(2,1)} %orb_hbm.1, bf16[112,128,128]{2,1,0:T(8,128)(2,1)} %tiles_hbm.1, bf16[32,2048]{1,0:T(8,128)(2,1)} %r_hbm.1), custom_call_target="tpu_custom_call" | custom-call | tf_op jit(solution)/shard_map/pallas_call | solution.py:444
  76.6 0.8 %copy.9 = bf16[32,8192]{1,0:T(8,128)(2,1)} copy(bf16[32,8192]{1,0:T(8,128)(2,1)S(1)} %shard_map.73) | data formatting | bytes 1048576

commit v4 on v3

--- a/solution.py
+++ b/solution.py
@@ -34,10 +34,10 @@
 
 
 def kernel(
-    rows_hbm, cols_hbm, counts_hbm, bounds_hbm, orb_hbm, tiles_hbm, r_hbm, out_hbm,
-    t_rows, t_cols, t_made, col_at, which_at, goes_on_at, last_at, counts, bounds, e0, e1, diag, extra, acc, seg, coef, f2, rv, rb, fb, ft, ob, ov,
-    in_sem, t_sem, h_send, h_recv, z_send, z_recv, x_send, x_recv,
-    f_send, f_recv, g_send, g_recv, o_send, o_recv, out_sem,
+    rows_hbm, cols_hbm, counts_hbm, bounds_hbm, orb_hbm, tiles_hbm, r_hbm, out,
+    t_rows, t_cols, t_made, col_at, which_at, goes_on_at, last_at, counts, bounds, e0, e1, diag, extra, acc, seg, coef, f2, rv, rb, fb, ft, ob,
+    in_sem, t_sem, h_send, h_recv, z_send, z_recv, x_send, x_recv, y_send, y_recv,
+    f_send, f_recv, g_send, g_recv, o_send, o_recv,
 ):
     s, o = lax.axis_index("slab"), lax.axis_index("orb")
     core, chip = lax.rem(o, 2), o // 2
@@ -46,6 +46,8 @@
     partner = o + 1 - 2 * core
     x_up, x_down = lax.rem(x + 1, NX), lax.rem(x + NX - 1, NX)
     x_far = lax.rem(x + 2, NX)
+    turn_of = lax.rem(s // 2, 2)
+    s_two_up, s_two_down = lax.rem(s + 2, N_SLAB), lax.rem(s + N_SLAB - 2, N_SLAB)
     s_up, s_down = lax.rem(s + 1, N_SLAB), lax.rem(s + N_SLAB - 1, N_SLAB)
     not_first, not_last = s > 0, s < N_SLAB - 1
 
@@ -94,9 +96,8 @@
             signal((near, lax.rem(chip + i, CHIPS) * 2 + x // 2))
         return carry
 
-    for near in (s_up, s_down):
-        for to in (o, partner):
-            signal((near, to))
+    for near in (s_up, s_down, s_two_up, s_two_down):
+        signal((near, o))
     lax.fori_loop(1, CHIPS, greet_chip, 0)
     lax.fori_loop(0, NZ, greet_column, 0)
     lax.fori_loop(0, jnp.where(same_parity & (core != x // 2), CHIPS, 0), greet_other, 0)
@@ -163,13 +164,14 @@
     def rotation_columns(to_core, step, to_z):
         return rv.at[:, aligned(column_group(to_core, half, step, to_z), TILE)]
 
-    def z_step(step, carry):
+    def z_step(i, carry):
+        step = jnp.where(i == 0, turn_of, i + 1)
         pltpu.make_async_copy(
             rotation_columns(core, step, z), rb.at[step, core, chip], z_recv.at[step]
         ).start()
 
-        def one(i, inner):
-            there = lax.rem(z * 2 + core + i, 2 * NZ)
+        def one(j, inner):
+            there = lax.rem(z * 2 + core + j, 2 * NZ)
             send(
                 rotation_columns(lax.rem(there, 2), step, there // 2),
                 rb.at[step, core, chip], z_send, z_recv.at[step], (s, x * 2 * NZ + there),
@@ -179,7 +181,7 @@
         lax.fori_loop(1, 2 * NZ, one, 0)
         return carry
 
-    lax.fori_loop(0, STEPS, z_step, 0)
+    lax.fori_loop(0, STEPS - 1, z_step, 0)
 
     def of_x(step, at_x):
         return rb.at[step, :, pl.ds(at_x * NZ, NZ)]
@@ -189,6 +191,11 @@
 
     def orb_at(at_x):
         return (at_x * NZ + z) * 2 + core
+
+    def to_slabs(step, at_x):
+        low, high = of_x_core(step, 0, at_x), of_x_core(step, 1, at_x)
+        send(low, low, y_send, y_recv, (s_two_up, o))
+        send(high, high, y_send, y_recv, (s_two_down, o))
 
     def stage_one(step):
         mine = of_x(step, x)
@@ -307,10 +314,11 @@
 
     lax.fori_loop(0, (BLOCKS - 2 * HB) // 4, inner_first, 0)
     apply_diagonal(e1)
-    stage_one(0)
+    stage_one(turn_of)
+    to_slabs(turn_of, x)
     wait_edges(e1, 1)
     apply_extra(e1)
-    stage_one(1)
+    stage_one(2)
 
     def destination(i):
         return lax.rem(x + i // NZ, NX) * NZ + lax.rem(z + lax.rem(i, NZ), NZ)
@@ -342,44 +350,56 @@
         at = pl.ds(at_x * NZ, NZ)
         got = fb.at[core, at, :, pl.ds(0, PAIR)]
         wait_bytes(got, f_recv.at[at_x])
-        for to in (o, partner):
-            send(fb.at[core, at, :, pl.ds(0, TILE)], fb.at[core, at, :, pl.ds(PAIR, TILE)],
-                 g_send, g_recv.at[at_x, 1], (s_up, to))
-            send(fb.at[core, at, :, pl.ds(TILE, TILE)], fb.at[core, at, :, pl.ds(PAIR + TILE, TILE)],
-                 g_send, g_recv.at[at_x, 2], (s_down, to))
+        send(fb.at[core, at, :, pl.ds(0, TILE)], fb.at[core, at, :, pl.ds(PAIR, TILE)],
+             g_send, g_recv.at[at_x, 1], (s_up, o))
+        send(fb.at[core, at, :, pl.ds(TILE, TILE)], fb.at[core, at, :, pl.ds(PAIR + TILE, TILE)],
+             g_send, g_recv.at[at_x, 2], (s_down, o))
         send(got, got, g_send, g_recv.at[at_x, 0], (s, partner))
         turn(core, at_x, 0)
         turn(core, at_x, TILE)
 
+    def relay(at_x):
+        at = pl.ds(at_x * NZ, NZ)
+        for side in range(2):
+            wait_bytes(fb.at[core, at, :, pl.ds(PAIR + side * TILE, TILE)], g_recv.at[at_x, 1 + side])
+        got = fb.at[core, at, :, pl.ds(PAIR, PAIR)]
+        send(got, got, g_send, g_recv.at[at_x, 3], (s, partner))
+        turn(core, at_x, PAIR)
+        turn(core, at_x, PAIR + TILE)
+
     def take(at_x):
         at = pl.ds(at_x * NZ, NZ)
-        wait_bytes(fb.at[1 - core, at, :, pl.ds(0, PAIR)], g_recv.at[at_x, 0])
-        turn(1 - core, at_x, 0)
-        turn(1 - core, at_x, TILE)
-        for side in range(2):
-            wait_bytes(fb.at[:, at, :, pl.ds(PAIR + side * TILE, TILE)], g_recv.at[at_x, 1 + side])
-            turn(0, at_x, PAIR + side * TILE)
-            turn(1, at_x, PAIR + side * TILE)
+        for part, which in ((0, 0), (1, 3)):
+            wait_bytes(fb.at[1 - core, at, :, pl.ds(part * PAIR, PAIR)], g_recv.at[at_x, which])
+            turn(1 - core, at_x, part * PAIR)
+            turn(1 - core, at_x, part * PAIR + TILE)
 
     def back_x(i):
         return lax.rem(x + NX - i, NX)
 
-    stage_one(2)
+    stage_two(turn_of)
+    to_slabs(turn_of, x_down)
+    to_slabs(turn_of, x_up)
     stage_one(3)
-    stage_two(0)
-    stage_two(1)
+    stage_two(2)
+    stage_three(turn_of)
+    to_slabs(turn_of, x_far)
     pass_on(back_x(0))
-    stage_three(0)
-    stage_two(2)
     pass_on(back_x(1))
-    stage_three(1)
+    relay(back_x(0))
     stage_two(3)
     pass_on(back_x(2))
+    relay(back_x(1))
     stage_three(2)
     pass_on(back_x(3))
-    for i in range(NX):
-        take(back_x(i))
+    relay(back_x(2))
+    take(back_x(0))
+    take(back_x(1))
+    relay(back_x(3))
+    take(back_x(2))
+    take(back_x(3))
     stage_three(3)
+    wait_bytes(rb.at[1 - turn_of], y_recv)
 
     def rotate(step, carry):
         slot = rb[step].reshape(2 * CHIPS * NORB_DEV, TILE)
@@ -392,25 +412,22 @@
         for i in range(4):
             rows = pl.ds(i * NORB_DEV, NORB_DEV)
             owner = first + i
-            send(ob.at[step, rows, pl.ds(PAIR, TILE)], ov.at[:, low], o_send, o_recv, (s_down, owner))
-            send(ob.at[step, rows, pl.ds(PAIR + TILE, TILE)], ov.at[:, high], o_send, o_recv, (s_up, owner))
+            send(ob.at[step, rows, pl.ds(PAIR, TILE)], out.at[:, low], o_send, o_recv, (s_down, owner))
+            send(ob.at[step, rows, pl.ds(PAIR + TILE, TILE)], out.at[:, high], o_send, o_recv, (s_up, owner))
             piece = ob.at[step, rows, pl.ds(0, PAIR)]
 
             @pl.when(owner == o)
             def _():
-                pltpu.make_async_copy(piece, ov.at[:, own], o_recv).start()
+                pltpu.make_async_copy(piece, out.at[:, own], o_recv).start()
 
             @pl.when(owner != o)
             def _():
-                send(piece, ov.at[:, own], o_send, o_recv, (s, owner))
+                send(piece, out.at[:, own], o_send, o_recv, (s, owner))
 
         return carry
 
     lax.fori_loop(0, STEPS, rotate, 0)
 
-    wait_bytes(ov, o_recv)
-    store = pltpu.make_async_copy(ov, out_hbm, out_sem)
-    store.start()
     for which, ext in ((0, e0), (1, e1)):
         @pl.when(not_last)
         def _():
@@ -420,8 +437,9 @@
         def _():
             wait_bytes(ext.at[high_edge], h_send.at[which, 1])
 
-    wait_bytes(rb.at[0, :, pl.ds(0, 30)], z_send)
-    wait_bytes(rb.at[pl.ds(0, 3)], x_send)
+    wait_bytes(rb.at[pl.ds(0, 3), 0, pl.ds(0, 15)], z_send)
+    wait_bytes(rb.at[pl.ds(0, 3), :, pl.ds(0, 24)], x_send)
+    wait_bytes(rb.at[0], y_send)
     wait_bytes(f2.at[pl.ds(0, CHIPS - 1)], f_send)
     wait_bytes(fb.at[:, :, :, pl.ds(0, PAIR + TILE)], g_send)
     mine_too = (x // 2 == core) & (lax.rem(z // 2, 2) == half)
@@ -434,7 +452,7 @@
     def _():
         wait_bytes(f2, o_send)
 
-    store.wait()
+    wait_bytes(out, o_recv)
 
 
 def local(orbitals_t, tiles, tile_rows, tile_cols, row_counts, bounds, rotation):
@@ -464,9 +482,8 @@
             pltpu.VMEM((2, CHIPS, NORB_DEV, 2 * PAIR), BF16),
             pltpu.VMEM((2 * PAIR, N_ORB * NORB_DEV), BF16),
             pltpu.VMEM((STEPS, TILE, 2 * PAIR), BF16),
-            pltpu.VMEM((NORB_DEV, ROWS_DEV), BF16),
-            dma((8,)), dma((4,)), dma((2, 2)), dma((2, 2)), dma, dma((STEPS,)), dma, dma((STEPS, 4)),
-            dma, dma((NX,)), dma, dma((NX, 3)), dma, dma, dma,
+            dma((8,)), dma((4,)), dma((2, 2)), dma((2, 2)), dma, dma((STEPS,)), dma, dma((STEPS, 4)), dma, dma,
+            dma, dma((NX,)), dma, dma((NX, 4)), dma, dma,
         ],
         compiler_params=pltpu.CompilerParams(
             collective_id=0, has_side_effects=True, vmem_limit_bytes=40 << 20

time: 77.5 us -> 72 us (0.929)
  Pallas kernels: 76.6 us -> 70.5 us
    pallas_call x1, Pallas kernels: 76.6 us -> 70.5 us  [local(): pl.pallas_call(kernel, out_shape=jax.ShapeDtypeStruct(orbitals_t.shape, B...]
where the time goes in v4:
time: 72 us; the launch traced here: 71.3 us
  Pallas kernels  70.5 us (98%)
  local copies, waits for them, and re-layouts  0.8 us (1%)
    pallas_call x1, Pallas kernels, local(): pl.pallas_call(kernel, out_shape=jax.ShapeDtypeStruct(orbitals_t.shape, B...  70.5 us

profile of v4, /device:TPU:1, one launch (start us, length us, event | category | flops | bytes accessed | tf_op | source)
XLA Modules:
  0.0 71.3 jit_solution(11074636988594703612)
XLA Ops:
  0.0 70.5 %shard_map.73 = bf16[32,8192]{1,0:T(8,128)(2,1)S(1)} custom-call(s32[1,112]{1,0:T(1,128)} %bitcast.2, s32[1,112]{1,0:T(1,128)} %bitcast.3, s32[64]{0:T(128)} %counts_hbm.1, f32[3]{0:T(128)} %bounds_hbm.1, bf16[32,8192]{1,0:T(8,128)(2,1)} %orb_hbm.1, bf16[112,128,128]{2,1,0:T(8,128)(2,1)} %tiles_hbm.1, bf16[32,2048]{1,0:T(8,128)(2,1)} %r_hbm.1), custom_call_target="tpu_custom_call" | custom-call | tf_op jit(solution)/shard_map/pallas_call | solution.py:462
  70.5 0.8 %copy.9 = bf16[32,8192]{1,0:T(8,128)(2,1)} copy(bf16[32,8192]{1,0:T(8,128)(2,1)S(1)} %shard_map.73) | data formatting | bytes 1048576

commit v5 on v4

--- a/solution.py
+++ b/solution.py
@@ -367,12 +367,11 @@
         turn(core, at_x, PAIR)
         turn(core, at_x, PAIR + TILE)
 
-    def take(at_x):
+    def take(at_x, part, which):
         at = pl.ds(at_x * NZ, NZ)
-        for part, which in ((0, 0), (1, 3)):
-            wait_bytes(fb.at[1 - core, at, :, pl.ds(part * PAIR, PAIR)], g_recv.at[at_x, which])
-            turn(1 - core, at_x, part * PAIR)
-            turn(1 - core, at_x, part * PAIR + TILE)
+        wait_bytes(fb.at[1 - core, at, :, pl.ds(part * PAIR, PAIR)], g_recv.at[at_x, which])
+        turn(1 - core, at_x, part * PAIR)
+        turn(1 - core, at_x, part * PAIR + TILE)
 
     def back_x(i):
         return lax.rem(x + NX - i, NX)
@@ -380,41 +379,37 @@
     stage_two(turn_of)
     to_slabs(turn_of, x_down)
     to_slabs(turn_of, x_up)
+    pass_on(back_x(0))
     stage_one(3)
     stage_two(2)
     stage_three(turn_of)
     to_slabs(turn_of, x_far)
-    pass_on(back_x(0))
     pass_on(back_x(1))
     relay(back_x(0))
-    stage_two(3)
     pass_on(back_x(2))
     relay(back_x(1))
-    stage_three(2)
+    stage_two(3)
     pass_on(back_x(3))
     relay(back_x(2))
-    take(back_x(0))
-    take(back_x(1))
-    relay(back_x(3))
-    take(back_x(2))
-    take(back_x(3))
-    stage_three(3)
-    wait_bytes(rb.at[1 - turn_of], y_recv)
-
-    def rotate(step, carry):
-        slot = rb[step].reshape(2 * CHIPS * NORB_DEV, TILE)
-        made = jnp.dot(ft[...], slot, preferred_element_type=F32)
-        ob[step] = made.T.astype(BF16)
+    stage_three(2)
+    for i in range(NX):
+        take(back_x(i), 0, 0)
+
+    own = pl.ds(pl.multiple_of(chip * PAIR, PAIR), PAIR)
+    low = pl.ds(pl.multiple_of(chip * PAIR, TILE), TILE)
+    high = pl.ds(pl.multiple_of(chip * PAIR + TILE, TILE), TILE)
+
+    def multiply(step, part):
+        slot = rb[step].reshape(N_ORB * NORB_DEV, TILE)
+        made = jnp.dot(ft[part * PAIR:(part + 1) * PAIR], slot, preferred_element_type=F32)
+        ob[step, :, part * PAIR:(part + 1) * PAIR] = made.T.astype(BF16)
+
+    def rotate_own(step):
+        multiply(step, 0)
         first = column_group(core, half, step, z) * 4
-        own = pl.ds(pl.multiple_of(chip * PAIR, PAIR), PAIR)
-        low = pl.ds(pl.multiple_of(chip * PAIR, TILE), TILE)
-        high = pl.ds(pl.multiple_of(chip * PAIR + TILE, TILE), TILE)
         for i in range(4):
-            rows = pl.ds(i * NORB_DEV, NORB_DEV)
             owner = first + i
-            send(ob.at[step, rows, pl.ds(PAIR, TILE)], out.at[:, low], o_send, o_recv, (s_down, owner))
-            send(ob.at[step, rows, pl.ds(PAIR + TILE, TILE)], out.at[:, high], o_send, o_recv, (s_up, owner))
-            piece = ob.at[step, rows, pl.ds(0, PAIR)]
+            piece = ob.at[step, pl.ds(i * NORB_DEV, NORB_DEV), pl.ds(0, PAIR)]
 
             @pl.when(owner == o)
             def _():
@@ -424,9 +419,25 @@
             def _():
                 send(piece, out.at[:, own], o_send, o_recv, (s, owner))
 
-        return carry
-
-    lax.fori_loop(0, STEPS, rotate, 0)
+    def rotate_near(step):
+        multiply(step, 1)
+        first = column_group(core, half, step, z) * 4
+        for i in range(4):
+            rows = pl.ds(i * NORB_DEV, NORB_DEV)
+            send(ob.at[step, rows, pl.ds(PAIR, TILE)], out.at[:, low], o_send, o_recv, (s_down, first + i))
+            send(ob.at[step, rows, pl.ds(PAIR + TILE, TILE)], out.at[:, high], o_send, o_recv, (s_up, first + i))
+
+    rotate_own(turn_of)
+    rotate_own(2)
+    relay(back_x(3))
+    stage_three(3)
+    rotate_own(3)
+    wait_bytes(rb.at[1 - turn_of], y_recv)
+    rotate_own(1 - turn_of)
+    for i in range(NX):
+        take(back_x(i), 1, 3)
+    for step in (turn_of, 2, 3, 1 - turn_of):
+        rotate_near(step)
 
     for which, ext in ((0, e0), (1, e1)):
         @pl.when(not_last)

time: 72 us -> 66.1 us (0.918)
  Pallas kernels: 70.5 us -> 64.8 us
    pallas_call x1, Pallas kernels: 70.5 us -> 64.8 us  [local(): pl.pallas_call(kernel, out_shape=jax.ShapeDtypeStruct(orbitals_t.shape, B...]
where the time goes in v5:
time: 66.1 us; the launch traced here: 65.6 us
  Pallas kernels  64.8 us (98%)
  local copies, waits for them, and re-layouts  0.8 us (1%)
    pallas_call x1, Pallas kernels, local(): pl.pallas_call(kernel, out_shape=jax.ShapeDtypeStruct(orbitals_t.shape, B...  64.8 us

profile of v5, /device:TPU:1, one launch (start us, length us, event | category | flops | bytes accessed | tf_op | source)
XLA Modules:
  0.0 65.6 jit_solution(7359253988156360613)
XLA Ops:
  0.0 64.8 %shard_map.73 = bf16[32,8192]{1,0:T(8,128)(2,1)S(1)} custom-call(s32[1,112]{1,0:T(1,128)} %bitcast.2, s32[1,112]{1,0:T(1,128)} %bitcast.3, s32[64]{0:T(128)} %counts_hbm.1, f32[3]{0:T(128)} %bounds_hbm.1, bf16[32,8192]{1,0:T(8,128)(2,1)} %orb_hbm.1, bf16[112,128,128]{2,1,0:T(8,128)(2,1)} %tiles_hbm.1, bf16[32,2048]{1,0:T(8,128)(2,1)} %r_hbm.1), custom_call_target="tpu_custom_call" | custom-call | tf_op jit(solution)/shard_map/pallas_call | solution.py:473
  64.8 0.8 %copy.9 = bf16[32,8192]{1,0:T(8,128)(2,1)} copy(bf16[32,8192]{1,0:T(8,128)(2,1)S(1)} %shard_map.73) | data formatting | bytes 1048576

commit v6 on v5

--- a/solution.py
+++ b/solution.py
@@ -127,94 +127,6 @@
 
     seg[EXTRA] = jnp.zeros((NORB_DEV, TILE), F32)
 
-    loads[2].wait()
-    wait_bytes(e0.at[pl.ds(HB, BLOCKS)], in_sem.at[5])
-    pl.semaphore_wait(barrier, 4 + (CHIPS - 1) + NZ + 8 + 32)
-
-    def send(src, dst, send_sem, recv_sem, to):
-        pltpu.make_async_remote_copy(
-            src_ref=src, dst_ref=dst, send_sem=send_sem, recv_sem=recv_sem,
-            device_id=to, device_id_type=MESH,
-        ).start()
-
-    low_edge, high_edge = pl.ds(0, HB), pl.ds(HB + BLOCKS, HB)
-
-    def send_edges(ext, which):
-        @pl.when(not_last)
-        def _():
-            send(ext.at[pl.ds(BLOCKS, HB)], ext.at[low_edge],
-                 h_send.at[which, 0], h_recv.at[which, 0], (s_up, o))
-
-        @pl.when(not_first)
-        def _():
-            send(ext.at[pl.ds(HB, HB)], ext.at[high_edge],
-                 h_send.at[which, 1], h_recv.at[which, 1], (s_down, o))
-
-    def wait_edges(ext, which):
-        @pl.when(not_first)
-        def _():
-            wait_bytes(ext.at[low_edge], h_recv.at[which, 0])
-
-        @pl.when(not_last)
-        def _():
-            wait_bytes(ext.at[high_edge], h_recv.at[which, 1])
-
-    send_edges(e0, 0)
-
-    def rotation_columns(to_core, step, to_z):
-        return rv.at[:, aligned(column_group(to_core, half, step, to_z), TILE)]
-
-    def z_step(i, carry):
-        step = jnp.where(i == 0, turn_of, i + 1)
-        pltpu.make_async_copy(
-            rotation_columns(core, step, z), rb.at[step, core, chip], z_recv.at[step]
-        ).start()
-
-        def one(j, inner):
-            there = lax.rem(z * 2 + core + j, 2 * NZ)
-            send(
-                rotation_columns(lax.rem(there, 2), step, there // 2),
-                rb.at[step, core, chip], z_send, z_recv.at[step], (s, x * 2 * NZ + there),
-            )
-            return inner
-
-        lax.fori_loop(1, 2 * NZ, one, 0)
-        return carry
-
-    lax.fori_loop(0, STEPS - 1, z_step, 0)
-
-    def of_x(step, at_x):
-        return rb.at[step, :, pl.ds(at_x * NZ, NZ)]
-
-    def of_x_core(step, at_core, at_x):
-        return rb.at[step, at_core, pl.ds(at_x * NZ, NZ)]
-
-    def orb_at(at_x):
-        return (at_x * NZ + z) * 2 + core
-
-    def to_slabs(step, at_x):
-        low, high = of_x_core(step, 0, at_x), of_x_core(step, 1, at_x)
-        send(low, low, y_send, y_recv, (s_two_up, o))
-        send(high, high, y_send, y_recv, (s_two_down, o))
-
-    def stage_one(step):
-        mine = of_x(step, x)
-        wait_bytes(mine, z_recv.at[step])
-        send(mine, mine, x_send, x_recv.at[step, 0], (s, orb_at(x_up)))
-        send(mine, mine, x_send, x_recv.at[step, 1], (s, orb_at(x_down)))
-
-    def stage_two(step):
-        wait_bytes(of_x(step, x_down), x_recv.at[step, 0])
-        relayed = of_x_core(step, 0, x_down)
-        send(relayed, relayed, x_send, x_recv.at[step, 2], (s, orb_at(x_up)))
-        wait_bytes(of_x(step, x_up), x_recv.at[step, 1])
-        relayed = of_x_core(step, 1, x_up)
-        send(relayed, relayed, x_send, x_recv.at[step, 3], (s, orb_at(x_down)))
-
-    def stage_three(step):
-        wait_bytes(of_x_core(step, 0, x_far), x_recv.at[step, 2])
-        wait_bytes(of_x_core(step, 1, x_far), x_recv.at[step, 3])
-
     table_copies = [
         pltpu.make_async_copy(t_made.at[pl.ds(i, 1)], to, t_sem.at[i])
         for i, to in enumerate((col_at, which_at, goes_on_at, last_at))
@@ -259,6 +171,99 @@
 
         lax.fori_loop(0, BLOCKS // UNROLL, body, 0)
 
+    loads[0].wait()
+    loads[5].wait()
+    make_table()
+    wait_bytes(e0.at[pl.ds(HB, BLOCKS)], in_sem.at[5])
+    loads[3].wait()
+    apply_diagonal(e0)
+    loads[2].wait()
+    pl.semaphore_wait(barrier, 4 + (CHIPS - 1) + NZ + 8 + 32)
+
+    def send(src, dst, send_sem, recv_sem, to):
+        pltpu.make_async_remote_copy(
+            src_ref=src, dst_ref=dst, send_sem=send_sem, recv_sem=recv_sem,
+            device_id=to, device_id_type=MESH,
+        ).start()
+
+    low_edge, high_edge = pl.ds(0, HB), pl.ds(HB + BLOCKS, HB)
+
+    def send_edges(ext, which):
+        @pl.when(not_last)
+        def _():
+            send(ext.at[pl.ds(BLOCKS, HB)], ext.at[low_edge],
+                 h_send.at[which, 0], h_recv.at[which, 0], (s_up, o))
+
+        @pl.when(not_first)
+        def _():
+            send(ext.at[pl.ds(HB, HB)], ext.at[high_edge],
+                 h_send.at[which, 1], h_recv.at[which, 1], (s_down, o))
+
+    def wait_edges(ext, which):
+        @pl.when(not_first)
+        def _():
+            wait_bytes(ext.at[low_edge], h_recv.at[which, 0])
+
+        @pl.when(not_last)
+        def _():
+            wait_bytes(ext.at[high_edge], h_recv.at[which, 1])
+
+    send_edges(e0, 0)
+
+    def rotation_columns(to_core, step, to_z):
+        return rv.at[:, aligned(column_group(to_core, half, step, to_z), TILE)]
+
+    def z_step(i, carry):
+        step = jnp.where(i == 0, turn_of, i + 1)
+        pltpu.make_async_copy(
+            rotation_columns(core, step, z), rb.at[step, core, chip], z_recv.at[step]
+        ).start()
+
+        def one(j, inner):
+            there = lax.rem(z * 2 + core + j, 2 * NZ)
+            send(
+                rotation_columns(lax.rem(there, 2), step, there // 2),
+                rb.at[step, core, chip], z_send, z_recv.at[step], (s, x * 2 * NZ + there),
+            )
+            return inner
+
+        lax.fori_loop(1, 2 * NZ, one, 0)
+        return carry
+
+    lax.fori_loop(0, STEPS - 1, z_step, 0)
+
+    def of_x(step, at_x):
+        return rb.at[step, :, pl.ds(at_x * NZ, NZ)]
+
+    def of_x_core(step, at_core, at_x):
+        return rb.at[step, at_core, pl.ds(at_x * NZ, NZ)]
+
+    def orb_at(at_x):
+        return (at_x * NZ + z) * 2 + core
+
+    def to_slabs(step, at_x):
+        low, high = of_x_core(step, 0, at_x), of_x_core(step, 1, at_x)
+        send(low, low, y_send, y_recv, (s_two_up, o))
+        send(high, high, y_send, y_recv, (s_two_down, o))
+
+    def stage_one(step):
+        mine = of_x(step, x)
+        wait_bytes(mine, z_recv.at[step])
+        send(mine, mine, x_send, x_recv.at[step, 0], (s, orb_at(x_up)))
+        send(mine, mine, x_send, x_recv.at[step, 1], (s, orb_at(x_down)))
+
+    def stage_two(step):
+        wait_bytes(of_x(step, x_down), x_recv.at[step, 0])
+        relayed = of_x_core(step, 0, x_down)
+        send(relayed, relayed, x_send, x_recv.at[step, 2], (s, orb_at(x_up)))
+        wait_bytes(of_x(step, x_up), x_recv.at[step, 1])
+        relayed = of_x_core(step, 1, x_up)
+        send(relayed, relayed, x_send, x_recv.at[step, 3], (s, orb_at(x_down)))
+
+    def stage_three(step):
+        wait_bytes(of_x_core(step, 0, x_far), x_recv.at[step, 2])
+        wait_bytes(of_x_core(step, 1, x_far), x_recv.at[step, 3])
+
     def apply_extra(ext):
         def multiply(i, carry):
             for u in range(UNROLL):
@@ -292,11 +297,6 @@
         value = (total - coef[0, 0:1] * first) * coef[2, 0:1] - coef[3, 0:1] * source
         return jnp.where(lanes < counts[b], value, 0.0).astype(BF16)
 
-    loads[0].wait()
-    loads[5].wait()
-    make_table()
-    loads[3].wait()
-    apply_diagonal(e0)
     loads[4].wait()
     for made in table_copies:
         made.wait()

time: 66.1 us -> 64.5 us (0.976)
  Pallas kernels: 64.8 us -> 63.3 us
    pallas_call x1, Pallas kernels: 64.8 us -> 63.3 us  [local(): pl.pallas_call(kernel, out_shape=jax.ShapeDtypeStruct(orbitals_t.shape, B...]
where the time goes in v6:
time: 64.5 us; the launch traced here: 64.1 us
  Pallas kernels  63.3 us (98%)
  local copies, waits for them, and re-layouts  0.8 us (1%)
    pallas_call x1, Pallas kernels, local(): pl.pallas_call(kernel, out_shape=jax.ShapeDtypeStruct(orbitals_t.shape, B...  63.3 us

profile of v6, /device:TPU:1, one launch (start us, length us, event | category | flops | bytes accessed | tf_op | source)
XLA Modules:
  0.0 64.1 jit_solution(4474473031223717931)
XLA Ops:
  0.0 63.3 %shard_map.73 = bf16[32,8192]{1,0:T(8,128)(2,1)S(1)} custom-call(s32[1,112]{1,0:T(1,128)} %bitcast.2, s32[1,112]{1,0:T(1,128)} %bitcast.3, s32[64]{0:T(128)} %counts_hbm.1, f32[3]{0:T(128)} %bounds_hbm.1, bf16[32,8192]{1,0:T(8,128)(2,1)} %orb_hbm.1, bf16[112,128,128]{2,1,0:T(8,128)(2,1)} %tiles_hbm.1, bf16[32,2048]{1,0:T(8,128)(2,1)} %r_hbm.1), custom_call_target="tpu_custom_call" | custom-call | tf_op jit(solution)/shard_map/pallas_call | solution.py:473
  63.3 0.8 %copy.9 = bf16[32,8192]{1,0:T(8,128)(2,1)} copy(bf16[32,8192]{1,0:T(8,128)(2,1)S(1)} %shard_map.73) | data formatting | bytes 1048576

commit v7 on v6

--- a/solution.py
+++ b/solution.py
@@ -18,7 +18,7 @@
 TILES = BLOCKS + EXTRA
 ROWS_DEV = BLOCKS * TILE
 STEPS = 4
-UNROLL = 8
+UNROLL = 16
 MESH = pl.DeviceIdType.MESH
 BF16, F32 = jnp.bfloat16, jnp.float32
 
@@ -391,7 +391,6 @@
     stage_two(3)
     pass_on(back_x(3))
     relay(back_x(2))
-    stage_three(2)
     for i in range(NX):
         take(back_x(i), 0, 0)
 
@@ -428,8 +427,9 @@
             send(ob.at[step, rows, pl.ds(PAIR + TILE, TILE)], out.at[:, high], o_send, o_recv, (s_up, first + i))
 
     rotate_own(turn_of)
+    relay(back_x(3))
+    stage_three(2)
     rotate_own(2)
-    relay(back_x(3))
     stage_three(3)
     rotate_own(3)
     wait_bytes(rb.at[1 - turn_of], y_recv)

time: 64.5 us -> 66.1 us (1.025)
  Pallas kernels: 63.3 us -> 65.2 us
    pallas_call x1, Pallas kernels: 63.3 us -> 65.2 us  [local(): pl.pallas_call(kernel, out_shape=jax.ShapeDtypeStruct(orbitals_t.shape, B...]
where the time goes in v7:
time: 66.1 us; the launch traced here: 66 us
  Pallas kernels  65.2 us (99%)
  local copies, waits for them, and re-layouts  0.8 us (1%)
    pallas_call x1, Pallas kernels, local(): pl.pallas_call(kernel, out_shape=jax.ShapeDtypeStruct(orbitals_t.shape, B...  65.2 us

profile of v7, /device:TPU:1, one launch (start us, length us, event | category | flops | bytes accessed | tf_op | source)
XLA Modules:
  0.0 66.0 jit_solution(15057269226368392948)
XLA Ops:
  0.0 65.2 %shard_map.73 = bf16[32,8192]{1,0:T(8,128)(2,1)S(1)} custom-call(s32[1,112]{1,0:T(1,128)} %bitcast.2, s32[1,112]{1,0:T(1,128)} %bitcast.3, s32[64]{0:T(128)} %counts_hbm.1, f32[3]{0:T(128)} %bounds_hbm.1, bf16[32,8192]{1,0:T(8,128)(2,1)} %orb_hbm.1, bf16[112,128,128]{2,1,0:T(8,128)(2,1)} %tiles_hbm.1, bf16[32,2048]{1,0:T(8,128)(2,1)} %r_hbm.1), custom_call_target="tpu_custom_call" | custom-call | tf_op jit(solution)/shard_map/pallas_call | solution.py:473
  65.2 0.8 %copy.9 = bf16[32,8192]{1,0:T(8,128)(2,1)} copy(bf16[32,8192]{1,0:T(8,128)(2,1)S(1)} %shard_map.73) | data formatting | bytes 1048576
